TPU v7x, 32 devices: a whole 2x2x4 slice. The times are simulated.
32 devices in a mesh: seq: 8 (over z, x), head: 4 (over y, core).
Axes of the slice: x: 2, y: 2, z: 4, core: 2. Of those that a mesh axis runs over, the one named last changes fastest.
Arguments:
- tokens: bfloat16 [8192, 768], P('seq'), may hold values from -6 to 6
- slide_ids: int32 [8192], P('seq'), may hold values from 0 to 3, never falling along the last dimension, each value on 1 to 4096 neighbouring positions
- valid: int32 [8192], P('seq'), may hold values 0 or 1
- norm_one: float32 [768], replicated, may hold values from 0.1 to 1.9
- w_qkv: bfloat16 [3, 768, 768], P(None, None, 'head'), may hold values from -0.21875 to 0.21875
- w_out: bfloat16 [768, 768], P('head'), may hold values from -2.5 to 2.5
- norm_two: float32 [768], replicated, may hold values from 0.1 to 1.9
- w_up: bfloat16 [768, 3072], P(None, 'head'), may hold values from -0.21875 to 0.21875
- w_down: bfloat16 [3072, 768], P('head'), may hold values from -0.109375 to 0.109375
- cotangent: bfloat16 [8192, 768], P('seq'), may hold values from -6 to 6
Outputs:
- output: bfloat16 [8192, 768], P('seq')
- input_grad: float32 [8192, 768], P('seq')
- grad_norm_one: float32 [768], replicated
- grad_qkv: float32 [3, 768, 768], P(None, None, 'head')
- grad_out: float32 [768, 768], P('head')
- grad_norm_two: float32 [768], replicated
- grad_up: float32 [768, 3072], P(None, 'head')
- grad_down: float32 [3072, 768], P('head')
Inputs may be any that keep to these rules, and one draw needn't show every extreme that they name: `slide_ids`: slide numbers never fall along the positions; each slide has 1 to 4096 positions, one exactly 4096.
All inputs are finite; a program needn't handle non-finite values. No bound on the sum of `valid` on one device may be relied on, other than what follows from the above.
Results may differ from a plain program's by a relative error of at most 0.019.
Values may be sent and summed in bfloat16 or wider, within the bound.
A program may use at most 192 MiB of HBM per device.

v0:
```python
from functools import partial

import jax
import jax.numpy as jnp
from jax import lax
from jax.sharding import PartitionSpec as P

HD = 48


seg_lengths = (1024, 2048, 4096, 8192, 16384)
ratios = (1, 2, 4, 8, 16)
eps = 1e-05
masked = -1e30


def for_sending(x):
    return jax.tree.map(lambda a: a.astype(jnp.bfloat16) if a.dtype == jnp.float32 else a, x)


def partner(block, axis, apart):
    count = lax.axis_size(axis)
    route = []
    for low in range(count):
        high = low | 1 << apart
        if high != low and high < count:
            route += [(low, high), (high, low)]
    return lax.ppermute(block, axis, route)


def normalize(rows_in, gain):
    centre = rows_in - jnp.mean(rows_in, axis=-1, keepdims=True)
    spread = jnp.mean(centre * centre, axis=-1, keepdims=True)
    return centre * lax.rsqrt(spread + eps) * gain


def select_rows(array, rate, offsets):
    amount = array.shape[0] // rate
    shaped = array.reshape((amount, rate) + array.shape[1:])
    chosen = (jnp.arange(rate, dtype=jnp.int32)[:, None] == offsets[None, :]).reshape(
        (1, rate, -1) + (1,) * (array.ndim - 2)
    )
    return jnp.sum(jnp.where(chosen, shaped, jnp.zeros((), array.dtype)), axis=1, dtype=array.dtype)


def place_rows(picked, rate, offsets, fill):
    amount = picked.shape[0]
    chosen = (jnp.arange(rate, dtype=jnp.int32)[:, None] == offsets[None, :]).reshape(
        (1, rate, -1) + (1,) * (picked.ndim - 2)
    )
    spread_out = jnp.where(chosen, picked[:, None], fill)
    return spread_out.reshape((amount * rate,) + picked.shape[1:])


def scores_of(queries, key_rows, query_tags, key_tags, factor):
    raw = jnp.einsum("qhd,khd->hqk", queries, key_rows, preferred_element_type=jnp.float32) * factor
    query_tag = query_tags.T[:, :, None]
    key_tag = key_tags.T[:, None, :]
    allowed = (query_tag // 2 == key_tag // 2) & ((key_tag % 2 == 1) | (query_tag % 2 == 0))
    return jnp.where(allowed, raw, masked)


def collect(kept, tag_kept, groups, again):
    position = lax.axis_index("seq")
    widest = max(groups)
    kept = list(kept)
    tag_kept = list(tag_kept)
    for level in range(widest.bit_length() - 1):
        active = [which for which in range(len(groups)) if groups[which] > 1 << level]
        lengths = [kept[which].shape[0] for which in active]
        packed = jnp.concatenate([kept[which] for which in active], axis=0)
        packed_tags = jnp.concatenate([tag_kept[which] for which in active], axis=0)
        if again:
            received, received_tags = (
                partner(packed, "seq", level),
                partner(for_sending(packed_tags), "seq", level).astype(packed_tags.dtype),
            )
        else:
            received, received_tags = (
                partner(packed, "seq", level),
                partner(for_sending(packed_tags), "seq", level).astype(packed_tags.dtype),
            )
        is_upper = position // (1 << level) % 2 == 1
        offset_row = 0
        for which, length in zip(active, lengths):
            theirs = received[offset_row : offset_row + length]
            their_tags = received_tags[offset_row : offset_row + length]
            kept[which] = jnp.where(
                is_upper,
                jnp.concatenate([theirs, kept[which]], axis=0),
                jnp.concatenate([kept[which], theirs], axis=0),
            )
            tag_kept[which] = jnp.where(
                is_upper,
                jnp.concatenate([their_tags, tag_kept[which]], axis=0),
                jnp.concatenate([tag_kept[which], their_tags], axis=0),
            )
            offset_row += length
    return (kept, tag_kept)


def return_grads(grads, groups):
    position = lax.axis_index("seq")
    widest = max(groups)
    grads = list(grads)
    for level in reversed(range(widest.bit_length() - 1)):
        active = [which for which in range(len(groups)) if groups[which] > 1 << level]
        is_upper = position // (1 << level) % 2 == 1
        keeping, sending, lengths = ([], [], [])
        for which in active:
            middle_row = grads[which].shape[0] // 2
            lower = grads[which][:middle_row]
            higher = grads[which][middle_row:]
            keeping.append(jnp.where(is_upper, higher, lower))
            sending.append(jnp.where(is_upper, lower, higher))
            lengths.append(middle_row)
        received = partner(for_sending(jnp.concatenate(sending, axis=0)), "seq", level)
        offset_row = 0
        for which, kept_part, length in zip(active, keeping, lengths):
            grads[which] = kept_part + received[offset_row : offset_row + length]
            offset_row += length
    return grads


def body(tokens, slide_ids, valid, norm_one, w_qkv, w_out, norm_two, w_up, w_down, cotangent):
    rows_here = tokens.shape[0]
    heads_here = w_out.shape[0] // HD
    total_rows = rows_here * lax.axis_size("seq")
    factor = HD ** (-0.5)
    first = tokens.astype(jnp.float32)
    normed, pull_one = jax.vjp(normalize, first, norm_one)
    normed_low = normed.astype(jnp.bfloat16)
    mixed = jnp.einsum("td,cde->cte", normed_low, w_qkv, preferred_element_type=jnp.float32).astype(
        jnp.bfloat16
    )
    query = mixed[0].reshape(rows_here, heads_here, HD)
    key_pairs = jnp.concatenate(
        [mixed[1].reshape(rows_here, heads_here, HD), mixed[2].reshape(rows_here, heads_here, HD)],
        axis=-1,
    )
    tags = 2 * slide_ids + valid
    head_tags = jnp.broadcast_to(tags[:, None], (rows_here, heads_here))
    head_base = lax.axis_index("head") * heads_here
    groups, offset_list, kept, tag_kept = ([], [], [], [])
    for seg, rate in zip(seg_lengths, ratios):
        groups.append(min(seg, total_rows) // rows_here)
        offsets = (head_base + jnp.arange(heads_here, dtype=jnp.int32)) % rate
        offset_list.append(offsets)
        kept.append(select_rows(key_pairs, rate, offsets))
        tag_kept.append(select_rows(head_tags, rate, offsets))
    gathered, gathered_tags = collect(kept, tag_kept, groups, False)
    parts, totals = ([], [])
    for which, rate in enumerate(ratios):
        offsets = offset_list[which]
        queries = select_rows(query, rate, offsets)
        scores = scores_of(
            queries, gathered[which][..., :HD], tag_kept[which], gathered_tags[which], factor
        )
        highest = jnp.max(scores, axis=-1, keepdims=True)
        log_total = highest + jnp.log(jnp.sum(jnp.exp(scores - highest), axis=-1, keepdims=True))
        weights = jnp.exp(scores - log_total).astype(jnp.bfloat16)
        result = jnp.einsum(
            "hqk,khd->qhd", weights, gathered[which][..., HD:], preferred_element_type=jnp.float32
        )
        parts.append(place_rows(result, rate, offsets, 0.0))
        totals.append(place_rows(log_total[:, :, 0].T, rate, offsets, masked))
    stacked = jnp.stack(totals)
    highest = jnp.max(stacked, axis=0)
    bound = highest + jnp.log(jnp.sum(jnp.exp(stacked - highest[None]), axis=0))
    attn_full = parts[0] * jnp.exp(totals[0] - bound)[:, :, None]
    for which in range(1, len(parts)):
        attn_full = attn_full + parts[which] * jnp.exp(totals[which] - bound)[:, :, None]
    attn_low = attn_full.reshape(rows_here, heads_here * HD).astype(jnp.bfloat16)
    attn_term = jnp.dot(attn_low, w_out, preferred_element_type=jnp.float32)
    middle = first + lax.psum(attn_term.astype(jnp.bfloat16), "head").astype(jnp.float32)
    second, pull_two = jax.vjp(normalize, middle, norm_two)
    second_low = second.astype(jnp.bfloat16)
    up_proj = jnp.dot(second_low, w_up, preferred_element_type=jnp.float32)
    hidden, pull_gelu = jax.vjp(partial(jax.nn.gelu, approximate=False), up_proj)
    hidden_low = hidden.astype(jnp.bfloat16)
    mlp_term = jnp.dot(hidden_low, w_down, preferred_element_type=jnp.float32)
    output = (middle + lax.psum(mlp_term.astype(jnp.bfloat16), "head").astype(jnp.float32)).astype(
        jnp.bfloat16
    )
    grad_down = jnp.einsum("tf,td->fd", hidden_low, cotangent, preferred_element_type=jnp.float32)
    d_hidden = jnp.einsum("td,fd->tf", cotangent, w_down, preferred_element_type=jnp.float32)
    d_up = pull_gelu(d_hidden)[0].astype(jnp.bfloat16)
    grad_up = jnp.einsum("td,tf->df", second_low, d_up, preferred_element_type=jnp.float32)
    d_second_term = jnp.einsum("tf,df->td", d_up, w_up, preferred_element_type=jnp.float32)
    d_second = lax.psum(d_second_term.astype(jnp.bfloat16), "head").astype(jnp.float32)
    d_middle_norm, grad_norm_two = pull_two(d_second)
    d_middle = cotangent.astype(jnp.float32) + d_middle_norm
    d_branch = d_middle.astype(jnp.bfloat16)
    grad_out = jnp.einsum("te,td->ed", attn_low, d_branch, preferred_element_type=jnp.float32)
    d_attn = jnp.einsum("td,ed->te", d_branch, w_out, preferred_element_type=jnp.float32).astype(
        jnp.bfloat16
    )
    d_attn = d_attn.reshape(rows_here, heads_here, HD)
    delta = jnp.sum(d_attn.astype(jnp.float32) * attn_full, axis=-1)
    pairs_back, tags_back = collect(kept, tag_kept, groups, True)
    d_query = jnp.zeros((rows_here, heads_here, HD), jnp.float32)
    d_pairs = []
    for which, rate in enumerate(ratios):
        offsets = offset_list[which]
        queries = select_rows(query, rate, offsets)
        key_rows = pairs_back[which][..., :HD]
        value_rows = pairs_back[which][..., HD:]
        scores = scores_of(queries, key_rows, tag_kept[which], tags_back[which], factor)
        bound_here = select_rows(bound, rate, offsets)
        delta_here = select_rows(delta, rate, offsets)
        d_attn_here = select_rows(d_attn, rate, offsets)
        probs = jnp.exp(scores - bound_here.T[:, :, None])
        d_probs = jnp.einsum(
            "qhd,khd->hqk", d_attn_here, value_rows, preferred_element_type=jnp.float32
        )
        d_scores = (probs * (d_probs - delta_here.T[:, :, None])).astype(jnp.bfloat16)
        d_query_here = (
            jnp.einsum("hqk,khd->qhd", d_scores, key_rows, preferred_element_type=jnp.float32)
            * factor
        )
        d_keys = (
            jnp.einsum("hqk,qhd->khd", d_scores, queries, preferred_element_type=jnp.float32)
            * factor
        )
        d_values = jnp.einsum(
            "hqk,qhd->khd",
            probs.astype(jnp.bfloat16),
            d_attn_here,
            preferred_element_type=jnp.float32,
        )
        d_pairs.append(jnp.concatenate([d_keys, d_values], axis=-1))
        d_query = d_query + place_rows(d_query_here, rate, offsets, 0.0)
    returned = return_grads(d_pairs, groups)
    d_pair_all = place_rows(returned[0], ratios[0], offset_list[0], 0.0)
    for which in range(1, len(ratios)):
        d_pair_all = d_pair_all + place_rows(
            returned[which], ratios[which], offset_list[which], 0.0
        )
    d_mixed = jnp.stack([d_query, d_pair_all[..., :HD], d_pair_all[..., HD:]]).reshape(
        3, rows_here, heads_here * HD
    )
    d_mixed = d_mixed.astype(jnp.bfloat16)
    grad_qkv = jnp.einsum("td,cte->cde", normed_low, d_mixed, preferred_element_type=jnp.float32)
    d_normed_term = jnp.einsum("cte,cde->td", d_mixed, w_qkv, preferred_element_type=jnp.float32)
    d_normed = lax.psum(d_normed_term.astype(jnp.bfloat16), "head").astype(jnp.float32)
    d_first, grad_norm_one = pull_one(d_normed)
    input_grad = d_middle + d_first
    summed = lax.psum((grad_norm_one, grad_qkv, grad_out, grad_norm_two, grad_up, grad_down), "seq")
    return (output, input_grad, summed[0], summed[1], summed[2], summed[3], summed[4], summed[5])


def solution(mesh):
    placed = (
        P("seq", None),
        P("seq"),
        P("seq"),
        P(),
        P(None, None, "head"),
        P("head", None),
        P(),
        P(None, "head"),
        P("head", None),
        P("seq", None),
    )
    return jax.shard_map(
        body,
        mesh=mesh,
        in_specs=placed,
        out_specs=(
            P("seq", None),
            P("seq", None),
            P(),
            P(None, None, "head"),
            P("head", None),
            P(),
            P(None, "head"),
            P("head", None),
        ),
        check_vma=False,
    )
```

profile of v0, /device:TPU:0, one launch (start us, length us, event | category | flops | bytes accessed | tf_op | source)
XLA Modules:
  0.0 943.6 jit_solution(11348384283820932260)
XLA Ops:
  36.0 3.5 fusion.81
  40.3 3.5 fusion.80
  43.9 3.8 fusion.79
  47.8 4.5 fusion.78
  77.3 8.6 fusion.154
  86.0 8.0 exponential_reduce_fusion
  151.3 5.7 fusion.70
  252.0 9.4 fusion.66
  263.8 4.7 add_convert_fusion.2
  281.2 4.8 copy.420
  286.0 4.8 copy.422
  290.8 3.9 copy.424
  354.9 9.4 add_convert_fusion
  375.0 36.1 %all-reduce.10.cloned.1.call-done = bf16[1024,768]{1,0:T(8,128)(2,1)} async-done(((bf16[1024,768]{1,0:T(8,128)(2,1)}), bf16[1024,768]{1,0:T(8,128)(2,1)}) %all-reduce.10.cloned.1.call-update) | async-done | bytes 1572880 | tf_op jit(solution)/shard_map/psum | solution.py:190
  411.2 4.4 fusion.23
  443.8 5.1 select_reduce_fusion.10
  452.8 5.8 fusion.59
  458.6 4.6 multiply_convert_fusion.1
  470.1 3.9 fusion.56
  490.0 8.0 multiply_convert_fusion
  500.8 4.0 convolution_multiply_fusion.4
  504.8 11.7 %collective-permute-done.6 = bf16[768,4,96]{0,2,1:T(8,128)(2,1)} collective-permute-done((bf16[768,4,96]{0,2,1:T(8,128)(2,1)}, bf16[768,4,96]{0,2,1:T(8,128)(2,1)}, u32[]{:S(2)}, u32[]{:S(2)}) %collective-permute-start.6) | collective-permute-done | bytes 589856 | tf_op jit(solution)/shard_map/ppermute | solution.py:28
  555.4 3.4 fusion.90
  558.9 7.0 fusion.65
  572.6 9.3 fusion.53
  582.0 8.4 collective-permute-done.8
  617.6 3.9 fusion.46
  624.6 4.9 fusion.157
  636.3 56.8 %all-reduce.14.cloned.1.call-done = (bf16[1024,768]{1,0:T(8,128)(2,1)}, bf16[1024,768]{1,0:T(8,128)(2,1)}) async-done(((bf16[1024,768]{1,0:T(8,128)(2,1)}, bf16[1024,768]{1,0:T(8,128)(2,1)}), (bf16[1024,768]{1,0:T(8,128)(2,1)}, bf16[1024,768]{1,0:T(8,128)(2,1)})) %all-reduce.14.cloned.1.call-update) | async-done | bytes 3145744 | tf_op jit(solution)/shard_map/psum | solution.py:182
  697.4 23.4 %all-reduce = (f32[768]{0:T(1024)}, f32[768]{0:T(1024)}) all-reduce(f32[768]{0:T(1024)S(1)} %get-tuple-element.10, f32[768]{0:T(1024)S(1)} %copy-done.179), channel_id=1, replica_groups=mesh['seq'=8,'head'=4] {'seq'}, use_global_device_ids=true, to_apply=%region_49.50 | all-reduce | flops 1536 | bytes 12288 | tf_op jit(solution)/shard_map/psum | solution.py:248
  720.9 6.1 add_add_fusion.2
  727.0 203.1 %all-reduce.12.cloned.1.call-done = (f32[3,768,192]{1,2,0:T(8,128)}, f32[192,768]{1,0:T(8,128)}, f32[768,768]{1,0:T(8,128)}, f32[768,768]{1,0:T(8,128)}) async-done(((f32[3,768,192]{1,2,0:T(8,128)}, f32[192,768]{1,0:T(8,128)}, f32[768,768]{1,0:T(8,128)}, f32[768,768]{1,0:T(8,128)}), (f32[3,768,192]{1,2,0:T(8,128)}, f32[192,768]{1,0:T(8,128)}, f32[768,768]{1,0:T(8,128)}, ...) | async-done | bytes 7077904 | tf_op jit(solution)/shard_map/psum | solution.py:248
  (792 shorter events, 442.5 us)
Async XLA Ops:
  7.2 347.2 %copy-start = (bf16[768,768]{1,0:T(8,128)(2,1)S(1)}, bf16[768,768]{1,0:T(8,128)(2,1)}, u32[]{:S(2)}) copy-start(bf16[768,768]{1,0:T(8,128)(2,1)} %param.18) | copy-start | bytes 3538948
  7.2 341.6 %all-reduce.8.cloned.1.call-start = ((), (), s32[]{:S(2)}) async-start(), calls=%async_computation | async-start | bytes 3145728 | tf_op jit(solution)/shard_map/psum | solution.py:175
  9.3 66.2 %copy-start.172 = (pred[2,4]{1,0:T(4,128)(4,1)}, pred[2,4]{1,0:T(4,128)(4,1)S(1)}, u32[]{:S(2)}) copy-start(pred[2,4]{1,0:T(4,128)(4,1)S(1)} %iota_compare_fusion.3) | copy-start | bytes 28
  9.4 60.3 %copy-start.183 = (pred[8,4]{1,0:T(8,128)(4,1)}, pred[8,4]{1,0:T(8,128)(4,1)S(1)}, u32[]{:S(2)}) copy-start(pred[8,4]{1,0:T(8,128)(4,1)S(1)} %iota_compare_fusion.1) | copy-start | bytes 100
  9.5 57.4 %copy-start.159 = (pred[16,4]{1,0:T(8,128)(4,1)}, pred[16,4]{1,0:T(8,128)(4,1)S(1)}, u32[]{:S(2)}) copy-start(pred[16,4]{1,0:T(8,128)(4,1)S(1)} %iota_compare_fusion) | copy-start | bytes 196
  12.8 43.4 %copy-start.161 = (s32[64,4]{0,1:T(4,128)}, s32[64,4]{0,1:T(4,128)S(1)}, u32[]{:S(2)}) copy-start(s32[64,4]{0,1:T(4,128)S(1)} %select_reduce_fusion.19) | copy-start | bytes 3076
  13.1 44.8 %copy-start.151 = (s32[256,4]{0,1:T(4,128)}, s32[256,4]{0,1:T(4,128)S(1)}, u32[]{:S(2)}) copy-start(s32[256,4]{0,1:T(4,128)S(1)} %select_reduce_fusion.12) | copy-start | bytes 12292
  13.8 102.9 %collective-permute-start = (s32[960,4]{0,1:T(4,128)}, s32[960,4]{0,1:T(4,128)}, u32[]{:S(2)}, u32[]{:S(2)}) collective-permute-start(s32[960,4]{0,1:T(4,128)} %pad_add_fusion), channel_id=1, source_target_pairs={{0,4},{4,0},{8,12},{12,8},{16,20},{20,16},{24,28},{28,24},{1,5},{5... | collective-permute-start | bytes 46088 | tf_op jit(solution)/shard_map/ppermute | solution.py:28
  55.6 75.1 %collective-permute-start.1 = (bf16[960,4,96]{0,2,1:T(8,128)(2,1)}, bf16[960,4,96]{0,2,1:T(8,128)(2,1)}, u32[]{:S(2)}, u32[]{:S(2)}) collective-permute-start(bf16[960,4,96]{0,2,1:T(8,128)(2,1)} %pad_maximum_fusion.4), channel_id=1, source_target_pairs={{0,4},{4,0},{8,12},{12,8},{16,20},{20,16},{24,28},{28,24},{1,5},{5... | collective-permute-start | bytes 2211848 | tf_op jit(solution)/shard_map/ppermute | solution.py:28
  94.0 23.4 %copy-start.162 = (s32[64,4]{0,1:T(4,128)S(1)}, s32[64,4]{0,1:T(4,128)}, u32[]{:S(2)}) copy-start(s32[64,4]{0,1:T(4,128)} %copy-done.161) | copy-start | bytes 3076
  94.0 24.8 %copy-start.152 = (s32[256,4]{0,1:T(4,128)S(1)}, s32[256,4]{0,1:T(4,128)}, u32[]{:S(2)}) copy-start(s32[256,4]{0,1:T(4,128)} %copy-done.151) | copy-start | bytes 12292
  95.2 38.4 %copy-start.101 = (pred[64,16,4]{1,0,2:T(8,128)(4,1)}, pred[64,16,4]{1,0,2:T(8,128)(4,1)S(1)}, u32[]{:S(2)}) copy-start(pred[64,16,4]{1,0,2:T(8,128)(4,1)S(1)} %broadcast_in_dim.920) | copy-start | bytes 12292
  95.4 38.3 %copy-start.125 = (pred[1024,4]{0,1:T(4,128)(4,1)}, pred[1024,4]{0,1:T(4,128)(4,1)S(1)}, u32[]{:S(2)}) copy-start(pred[1024,4]{0,1:T(4,128)(4,1)S(1)} %broadcast_in_dim.950) | copy-start | bytes 12292
  95.4 38.3 %copy-start.99 = (bf16[128,4,96]{0,2,1:T(8,128)(2,1)S(1)}, bf16[128,4,96]{0,2,1:T(8,128)(2,1)}, u32[]{:S(2)}) copy-start(bf16[128,4,96]{0,2,1:T(8,128)(2,1)} %copy-done.98) | copy-start | bytes 294916
  96.2 37.5 %copy-start.128 = (pred[1024,4]{0,1:T(4,128)(4,1)}, pred[1024,4]{0,1:T(4,128)(4,1)S(1)}, u32[]{:S(2)}) copy-start(pred[1024,4]{0,1:T(4,128)(4,1)S(1)} %broadcast_in_dim.944) | copy-start | bytes 12292
  96.6 38.2 %copy-start.131 = (pred[1024,4]{0,1:T(4,128)(4,1)}, pred[1024,4]{0,1:T(4,128)(4,1)S(1)}, u32[]{:S(2)}) copy-start(pred[1024,4]{0,1:T(4,128)(4,1)S(1)} %broadcast_in_dim.938) | copy-start | bytes 12292
  98.5 36.4 %copy-start.53 = (bf16[512,4,96]{0,2,1:T(8,128)(2,1)S(1)}, bf16[512,4,96]{0,2,1:T(8,128)(2,1)}, u32[]{:S(2)}) copy-start(bf16[512,4,96]{0,2,1:T(8,128)(2,1)} %copy-done.52) | copy-start | bytes 1179652
  107.2 29.2 %copy-start.134 = (pred[1024,4]{0,1:T(4,128)(4,1)}, pred[1024,4]{0,1:T(4,128)(4,1)S(1)}, u32[]{:S(2)}) copy-start(pred[1024,4]{0,1:T(4,128)(4,1)S(1)} %copy.475) | copy-start | bytes 12292
  119.6 19.8 %copy-start.86 = (bf16[512,4,48]{0,2,1:T(8,128)(2,1)S(1)}, bf16[512,4,48]{0,2,1:T(8,128)(2,1)}, u32[]{:S(2)}) copy-start(bf16[512,4,48]{0,2,1:T(8,128)(2,1)} %copy.379) | copy-start | bytes 589828
  119.6 19.8 %copy-start.187 = (s32[4,512]{1,0:T(4,128)S(1)}, s32[4,512]{1,0:T(4,128)}, u32[]{:S(2)}) copy-start(s32[4,512]{1,0:T(4,128)} %add_select_fusion.13) | copy-start | bytes 24580
  119.6 3.9 collective-permute-start.2
  123.5 4.8 collective-permute-start.4
  137.4 28.6 %collective-permute-start.3 = (bf16[896,4,96]{0,2,1:T(8,128)(2,1)}, bf16[896,4,96]{0,2,1:T(8,128)(2,1)}, u32[]{:S(2)}, u32[]{:S(2)}) collective-permute-start(bf16[896,4,96]{0,2,1:T(8,128)(2,1)} %pad_maximum_fusion.6), channel_id=1, source_target_pairs={{0,8},{8,0},{4,12},{12,4},{16,24},{24,16},{20,28},{28,20},{1,9},{9... | collective-permute-start | bytes 2064392 | tf_op jit(solution)/shard_map/ppermute | solution.py:28
  172.7 25.8 %collective-permute-start.5 = (bf16[768,4,96]{0,2,1:T(8,128)(2,1)}, bf16[768,4,96]{0,2,1:T(8,128)(2,1)}, u32[]{:S(2)}, u32[]{:S(2)}) collective-permute-start(bf16[768,4,96]{0,2,1:T(8,128)(2,1)} %pad_maximum_fusion.8), channel_id=1, source_target_pairs={{0,16},{16,0},{4,20},{20,4},{8,24},{24,8},{12,28},{28,12},{1,17},{... | collective-permute-start | bytes 1769480 | tf_op jit(solution)/shard_map/ppermute | solution.py:28
  271.1 140.1 %all-reduce.10.cloned.1.call-start = ((), (), s32[]{:S(2)}) async-start(), calls=%async_computation.1 | async-start | bytes 3145728 | tf_op jit(solution)/shard_map/psum | solution.py:190
  368.0 325.0 %all-reduce.14.cloned.1.call-start = ((), (), s32[]{:S(2)}) async-start(), calls=%async_computation.3 | async-start | bytes 6291456 | tf_op jit(solution)/shard_map/psum | solution.py:182
  487.6 28.8 %collective-permute-start.6 = (bf16[768,4,96]{0,2,1:T(8,128)(2,1)}, bf16[768,4,96]{0,2,1:T(8,128)(2,1)}, u32[]{:S(2)}, u32[]{:S(2)}) collective-permute-start(bf16[768,4,96]{0,2,1:T(8,128)(2,1)} %pad_maximum_fusion.9), channel_id=1, source_target_pairs={{0,16},{16,0},{4,20},{20,4},{8,24},{24,8},{12,28},{28,12},{1,17},{... | collective-permute-start | bytes 1769480 | tf_op jit(solution)/shard_map/ppermute | solution.py:28
  521.4 44.4 %collective-permute-start.7 = (bf16[896,4,96]{0,2,1:T(8,128)(2,1)}, bf16[896,4,96]{0,2,1:T(8,128)(2,1)}, u32[]{:S(2)}, u32[]{:S(2)}) collective-permute-start(bf16[896,4,96]{0,2,1:T(8,128)(2,1)} %pad_maximum_fusion.7), channel_id=1, source_target_pairs={{0,8},{8,0},{4,12},{12,4},{16,24},{24,16},{20,28},{28,20},{1,9},{9... | collective-permute-start | bytes 2064392 | tf_op jit(solution)/shard_map/ppermute | solution.py:28
  571.1 19.2 %collective-permute-start.8 = (bf16[960,4,96]{0,2,1:T(8,128)(2,1)S(1)}, bf16[960,4,96]{0,2,1:T(8,128)(2,1)S(1)}, u32[]{:S(2)}, u32[]{:S(2)}) collective-permute-start(bf16[960,4,96]{0,2,1:T(8,128)(2,1)S(1)} %pad_maximum_fusion.5), channel_id=1, source_target_pairs={{0,4},{4,0},{8,12},{12,8},{16,20},{20,16},{24,28},{28,24},{1,5},{5... | collective-permute-start | bytes 2211848 | tf_op jit(solution)/shard_map/ppermute | solution.py:28
  624.3 305.7 %all-reduce.12.cloned.1.call-start = ((), (), s32[]{:S(2)}) async-start(), calls=%async_computation.2 | async-start | bytes 14155776 | tf_op jit(solution)/shard_map/psum | solution.py:248
  636.2 59.2 %copy-start.165 = (f32[1024]{0:T(1024)S(1)}, f32[1024]{0:T(1024)}, u32[]{:S(2)}) copy-start(f32[1024]{0:T(1024)} %copy-done.164) | copy-start | bytes 12292
  693.0 27.8 %copy-start.171 = (f32[1024]{0:T(1024)S(1)}, f32[1024]{0:T(1024)}, u32[]{:S(2)}) copy-start(f32[1024]{0:T(1024)} %copy-done.170) | copy-start | bytes 12292
  (191 other events, 1068.7 us)
Sparse Core Ops, SparseCore 0:
  271.2 42.9 all-reduce.7
  368.2 42.9 all-reduce.9
  624.4 68.5 all-reduce.13
  697.9 232.0 all-reduce.11
where the time goes:
time: 958 us; the launch traced here: 944 us
  waiting for transfers between devices  320 us (33%)
  local copies, waits for them, and re-layouts  294 us (31%)
  other arithmetic  142 us (15%)
  matrix products  129 us (13%)
  blocking collectives  23.4 us (2%)
  starting transfers between devices  18.1 us (2%)
  between operations  16.9 us (2%)
    psum x1, waiting for transfers between devices, body(): lax.psum((grad_norm_one, grad_qkv, grad_out, grad_norm_two, grad_up, grad...  203 us
    broadcast_in_dim x56, local copies, waits for them, and re-layouts, place_rows(): spread_out = jnp.where(chosen, picked[:, None], fill)  117 us
    psum x1, waiting for transfers between devices, body(): lax.psum(mlp_term.astype(jnp.bfloat16), 'head').astype(jnp.float32)  56.8 us
    reduce_sum x20, other arithmetic, select_rows(): jnp.sum(jnp.where(chosen, shaped, jnp.zeros((), array.dtype)), axis=1, dt...  46.3 us
    psum x1, waiting for transfers between devices, body(): lax.psum(d_second_term.astype(jnp.bfloat16), 'head').astype(jnp.float32)  36.1 us
    unnamed x433, local copies, waits for them, and re-layouts  35.5 us
    broadcast_in_dim x23, local copies, waits for them, and re-layouts, select_rows(): jnp.where(chosen, shaped, jnp.zeros((), array.dtype))  29.1 us
    ppermute x9, waiting for transfers between devices, partner(): return lax.ppermute(block, axis, route)  24.3 us
  transfers between devices with their start and end apart: 13, of which 8 were waited for; matrix products, arithmetic and copies ran while one was open for 34% of the time, Pallas kernels for 0%

commit v1 on v0

v1 whole, which is shorter than its diff:
```python
from functools import partial

import jax
import jax.numpy as jnp
from jax import lax
from jax.experimental import pallas as pl
from jax.experimental.pallas import tpu as pltpu
from jax.sharding import PartitionSpec as P

HD = 48
SLOT = 64
CLASSES = 16
CHUNK = CLASSES * 16
EPS = 1e-05
NEG = -(2.0**30)
LOG2E = 1.4426950408889634
FACTOR = HD ** (-0.5)
MESH = pl.DeviceIdType.MESH
f32 = jnp.float32
bf16 = jnp.bfloat16
NT = (((1,), (1,)), ((), ()))
VMEM = pl.BlockSpec(memory_space=pltpu.VMEM)
LIMIT = 60 * 1024 * 1024


def dot(a, b):
    return jnp.dot(a, b, preferred_element_type=f32)


def dot_nt(a, b):
    return lax.dot_general(a, b, NT, preferred_element_type=f32)


def iota(shape, dim):
    return lax.broadcasted_iota(jnp.int32, shape, dim)


def one_hot(cond):
    return jnp.where(cond, 1.0, 0.0).astype(bf16)


def digit_swap():
    row, col = iota((CHUNK, CHUNK), 0), iota((CHUNK, CHUNK), 1)
    return one_hot(col == 16 * (row % 16) + row // 16)


def spreader(width):
    row, col = iota((width, width // HD * SLOT), 0), iota((width, width // HD * SLOT), 1)
    return one_hot(col == SLOT * (row // HD) + row % HD)


def unspreader(width):
    row, col = iota((width // HD * SLOT, width), 0), iota((width // HD * SLOT, width), 1)
    return one_hot(row == SLOT * (col // HD) + col % HD)


def eye(size):
    return one_hot(iota((size, size), 0) == iota((size, size), 1))


def bit_reverse(i):
    return i % 2 * 8 + i // 2 % 2 * 4 + i // 4 % 2 * 2 + i // 8


def peer_of(me, apart):
    out = me
    for bit in range(apart.bit_length()):
        if apart >> bit & 1:
            out = out + (1 << bit) * (1 - 2 * (me // (1 << bit) % 2))
    return out


def level_count(n_seq):
    count = 0
    while count < 4 and 2 << count <= n_seq:
        count += 1
    return count


def slots_of(level, half):
    rows = half >> level
    return [
        (apart, level * half + (apart - (1 << level)) * rows, rows)
        for apart in range(1 << level, 2 << level)
    ]


def depth_of(index, half):
    total = jnp.zeros(index.shape, f32)
    for level in range(4):
        total = total + jnp.where(index < half >> level, 1.0, 0.0)
    return total


def pair_counts(keys, queries, half, level):
    period = half if level is None else half >> level
    key = depth_of(iota((keys, queries), 0) % period, half)
    query = depth_of(iota((keys, queries), 1), half)
    return jnp.minimum(key, query) + (1.0 if level is None else -1.0 * level)


def greet(peers, axis):
    barrier = pltpu.get_barrier_semaphore()
    for peer in peers:
        pl.semaphore_signal(barrier, inc=1, device_id={axis: peer}, device_id_type=MESH)
    pl.semaphore_wait(barrier, len(peers))


def half_mask(which, rows):
    lane = iota((rows, 2 * SLOT), 1)
    return one_hot(lane // SLOT == which)


def to_classes(value, t, cls_ref, lanes, block):
    for c in range(CLASSES):
        start = pl.multiple_of(c * block + t * 16, 16)
        cls_ref[pl.ds(start, 16), lanes] = value[16 * c : 16 * c + 16]


def class_start(i, head, block):
    return pl.multiple_of((bit_reverse(i) + head) % CLASSES * block, block)


def place_start(c, head, block):
    return pl.multiple_of(bit_reverse((c + CLASSES - head) % CLASSES) * block, block)


def from_heads(src_refs, base, dst_ref, block):
    low = iota((block, 2 * SLOT), 1) < SLOT

    def step(c, carry):
        for tile, (ref, pair) in enumerate(src_refs):
            left = ref[pair, pl.ds(place_start(c, base + 2 * pair, block), block), :]
            right = ref[pair, pl.ds(place_start(c, base + 2 * pair + 1, block), block), :]
            both = jnp.where(low, left, right).astype(bf16)
            for t in range(block // 16):
                start = pl.multiple_of(t * CHUNK + c * 16, 16)
                dst_ref[pl.ds(start, 16), tile * 128 : tile * 128 + 128] = both[16 * t : 16 * t + 16]
        return carry

    lax.fori_loop(0, CLASSES, step, 0)


def project_kernel(heads, tokens_ref, aux_ref, gain_ref, w_ref, normed_ref, qz_ref, kv_ref, cls_ref):
    rows = tokens_ref.shape[0]
    block = rows // CLASSES
    width = heads * HD
    wide = heads * SLOT
    swap = digit_swap()
    spread = spreader(width)
    ones = jnp.where(iota((CHUNK, wide), 1) % SLOT >= HD, 1.0, 0.0)

    def step(t, carry):
        here = pl.ds(pl.multiple_of(t * CHUNK, CHUNK), CHUNK)
        x = tokens_ref[here, :].astype(f32)
        centre = x - jnp.mean(x, axis=-1, keepdims=True)
        spread_of = jnp.mean(centre * centre, axis=-1, keepdims=True)
        normed = (centre * lax.rsqrt(spread_of + EPS) * gain_ref[...]).astype(bf16)
        normed_ref[here, :] = normed
        for c in range(3):
            y = dot(normed, w_ref[c])
            if c == 1:
                y = y * (FACTOR * LOG2E)
            y = dot(y.astype(bf16), spread)
            if c < 2:
                y = y + aux_ref[here, c * wide : c * wide + wide].astype(f32)
            else:
                y = y + ones
            y = dot(swap, y.astype(bf16)).astype(bf16)
            to_classes(y, t, cls_ref, slice(c * wide, c * wide + wide), block)
        return carry

    lax.fori_loop(0, rows // CHUNK, step, 0)
    base = lax.axis_index("head") * heads
    masks = [half_mask(0, block), half_mask(1, block)]

    def pick(i, carry):
        out = pl.ds(pl.multiple_of(i * block, block), block)
        for j in range(heads):
            src = pl.ds(class_start(i, base + j, block), block)
            lanes = slice(j // 2 * 128, j // 2 * 128 + 128)
            qz_ref[j, out, :] = cls_ref[src, lanes] * masks[j % 2]
        for tile in range(heads):
            pair = tile % (heads // 2)
            lanes = slice(wide + tile * 128, wide + tile * 128 + 128)
            left = cls_ref[pl.ds(class_start(i, base + 2 * pair, block), block), lanes]
            right = cls_ref[pl.ds(class_start(i, base + 2 * pair + 1, block), block), lanes]
            kv_ref[tile, out, :] = left * masks[0] + right * masks[1]
        return carry

    lax.fori_loop(0, CLASSES, pick, 0)


def transpose_heads(ref, first, start, count, out_ref, heads):
    unit = eye(2 * SLOT)
    for pair in range(heads // 2):
        turned = dot_nt(unit, ref[first + pair, start : start + count, :]).astype(bf16)
        out_ref[2 * pair, :, :count] = turned[:SLOT]
        out_ref[2 * pair + 1, :, :count] = turned[SLOT:]


def attend_kernel(
    levels, heads, qz_ref, kv_ref, attn_ref, attn_t_ref, bound_ref, rk_ref,
    vt_ref, s_ref, p_ref, acc_ref, m_ref, a_ref, d_ref, send_sem, recv_sem,
):
    rows = kv_ref.shape[1]
    half = rows // 2
    block = rows // CLASSES
    me = lax.axis_index("seq")
    slots = [slot for level in range(levels) for slot in slots_of(level, half)]
    greet([peer_of(me, apart) for apart, _, _ in slots], "seq")
    copies = {}
    for apart, offset, count in slots:
        copies[apart] = pltpu.make_async_remote_copy(
            src_ref=kv_ref.at[:, 0:count, :],
            dst_ref=rk_ref.at[:, offset : offset + count, :],
            send_sem=send_sem.at[apart - 1],
            recv_sem=recv_sem.at[apart - 1],
            device_id={"seq": peer_of(me, apart)},
            device_id_type=MESH,
        )
        copies[apart].start()
    transpose_heads(kv_ref, heads // 2, 0, rows, vt_ref, heads)

    def local(pair, carry):
        counts = pair_counts(half, half, half, None)
        for qt in range(2):
            there = slice(qt * half, qt * half + half)
            for side in range(2):
                h = 2 * pair + side
                s_ref[side] = dot_nt(kv_ref[pair], qz_ref[h, there, :])
                top = jnp.max(s_ref[side], axis=0, keepdims=True)
                low = jnp.exp2(s_ref[side, :half] - top)
                if qt == 0:
                    low = low * counts
                p_ref[side, :half] = low.astype(bf16)
                p_ref[side, half:] = jnp.exp2(s_ref[side, half:] - top).astype(bf16)
                acc_ref[h, :, there] = dot(vt_ref[h], p_ref[side])
                m_ref[h, :, there] = top
        return carry

    lax.fori_loop(0, heads // 2, local, 0)

    for level in range(levels):
        queries = max(half >> level, 128)
        for apart, _, _ in slots_of(level, half):
            copies[apart].wait_recv()
        keys = slice(level * half, level * half + half)
        transpose_heads(rk_ref, heads // 2, level * half, half, vt_ref, heads)

        def remote(pair, carry):
            counts = pair_counts(half, queries, half, level)
            for side in range(2):
                h = 2 * pair + side
                s = dot_nt(rk_ref[pair, keys, :], qz_ref[h, :queries, :])
                if half >> level < queries:
                    s = s + jnp.where(counts > 0.0, 0.0, NEG)
                old = m_ref[h, :, :queries]
                top = jnp.maximum(old, jnp.max(s, axis=0, keepdims=True))
                p = (jnp.exp2(s - top) * counts).astype(bf16)
                acc_ref[h, :, :queries] = acc_ref[h, :, :queries] * jnp.exp2(old - top) + dot(
                    vt_ref[h, :, :half], p
                )
                m_ref[h, :, :queries] = top
            return carry

        lax.fori_loop(0, heads // 2, remote, 0)

    for h in range(heads):
        total = acc_ref[h, HD : HD + 1, :]
        bound_ref[h] = m_ref[h] + jnp.log2(total)
        attn_t_ref[h] = acc_ref[h] * (1.0 / total)
    for pair in range(heads // 2):
        a_ref[pair] = jnp.concatenate([attn_t_ref[2 * pair], attn_t_ref[2 * pair + 1]], axis=0).T
    base = lax.axis_index("head") * heads
    from_heads([(a_ref, pair) for pair in range(heads // 2)], base, d_ref, block)
    swap = digit_swap()
    unspread = unspreader(heads * HD)
    for t in range(rows // CHUNK):
        here = slice(t * CHUNK, t * CHUNK + CHUNK)
        natural = dot(swap, d_ref[here, :]).astype(bf16)
        attn_ref[here, :] = dot(natural, unspread).astype(bf16)
    for apart, _, _ in slots:
        copies[apart].wait_send()


def attend_back_kernel(
    levels, heads, qz_ref, kv_ref, rk_ref, da_ref, attn_t_ref, bound_ref, dmixed_ref,
    cls_ref, doz_ref, delta_ref, kt_ref, p_ref, ds_ref, dkv_ref, dqt_ref, dq_ref, sb_ref, rg_ref, d_ref,
    send_sem, recv_sem,
):
    rows = kv_ref.shape[1]
    half = rows // 2
    block = rows // CLASSES
    pairs = heads // 2
    wide = heads * SLOT
    me = lax.axis_index("seq")
    base = lax.axis_index("head") * heads
    slots = [slot for level in range(levels) for slot in slots_of(level, half)]
    greet([peer_of(me, apart) for apart, _, _ in slots], "seq")
    swap = digit_swap()
    spread = spreader(heads * HD)
    for t in range(rows // CHUNK):
        y = dot(da_ref[t * CHUNK : t * CHUNK + CHUNK, :], spread).astype(bf16)
        y = dot(swap, y).astype(bf16)
        to_classes(y, t, cls_ref, slice(0, wide), block)
    masks = [half_mask(0, block), half_mask(1, block)]

    def pick(i, carry):
        out = pl.ds(pl.multiple_of(i * block, block), block)
        for j in range(heads):
            src = pl.ds(class_start(i, base + j, block), block)
            lanes = slice(j // 2 * 128, j // 2 * 128 + 128)
            doz_ref[j, out, :] = cls_ref[src, lanes] * masks[j % 2]
        return carry

    lax.fori_loop(0, CLASSES, pick, 0)
    unit = eye(2 * SLOT)
    for h in range(heads):
        turned = dot_nt(unit, doz_ref[h])[h % 2 * SLOT : h % 2 * SLOT + SLOT]
        delta_ref[h] = jnp.sum(turned * attn_t_ref[h], axis=0, keepdims=True)

    dqt_ref[...] = jnp.zeros_like(dqt_ref)
    copies = {}
    for level in range(levels):
        queries = max(half >> level, 128)
        keys = slice(level * half, level * half + half)
        transpose_heads(rk_ref, 0, level * half, half, kt_ref, heads)

        def remote(pair, carry):
            counts = pair_counts(half, queries, half, level)
            dk = jnp.zeros((half, 128), f32)
            dv = jnp.zeros((half, 128), f32)
            for side in range(2):
                h = 2 * pair + side
                q, do = qz_ref[h, :queries, :], doz_ref[h, :queries, :]
                p = jnp.exp2(dot_nt(rk_ref[pair, keys, :], q) - bound_ref[h, :, :queries]) * counts
                ds = p * (dot_nt(rk_ref[pairs + pair, keys, :], do) - delta_ref[h, :, :queries])
                p, ds = p.astype(bf16), ds.astype(bf16)
                dv = dv + dot(p, do)
                dk = dk + dot(ds, q)
                dqt_ref[h, :, :queries] += dot(kt_ref[h, :, :half], ds)
            sb_ref[pair, keys, :] = dk.astype(bf16)
            sb_ref[pairs + pair, keys, :] = dv.astype(bf16)
            return carry

        lax.fori_loop(0, pairs, remote, 0)
        for apart, offset, count in slots_of(level, half):
            copies[apart] = pltpu.make_async_remote_copy(
                src_ref=sb_ref.at[:, offset : offset + count, :],
                dst_ref=rg_ref.at[:, offset : offset + count, :],
                send_sem=send_sem.at[apart - 1],
                recv_sem=recv_sem.at[apart - 1],
                device_id={"seq": peer_of(me, apart)},
                device_id_type=MESH,
            )
            copies[apart].start()

    transpose_heads(kv_ref, 0, 0, rows, kt_ref, heads)

    def local(pair, carry):
        counts = pair_counts(half, half, half, None)
        for qt in range(2):
            there = slice(qt * half, qt * half + half)
            for side in range(2):
                h = 2 * pair + side
                q, do = qz_ref[h, there, :], doz_ref[h, there, :]
                for kt in range(2):
                    keys = slice(kt * half, kt * half + half)
                    p = jnp.exp2(dot_nt(kv_ref[pair, keys, :], q) - bound_ref[h, :, there])
                    if qt == 0 and kt == 0:
                        p = p * counts
                    ds = p * (dot_nt(kv_ref[pairs + pair, keys, :], do) - delta_ref[h, :, there])
                    p_ref[side, keys, :] = p.astype(bf16)
                    ds_ref[side, keys, :] = ds.astype(bf16)
                dv = dot(p_ref[side], do)
                dk = dot(ds_ref[side], q)
                if qt == 0 and side == 0:
                    dkv_ref[pairs + pair] = dv
                    dkv_ref[pair] = dk
                else:
                    dkv_ref[pairs + pair] += dv
                    dkv_ref[pair] += dk
                dqt_ref[h, :, there] += dot(kt_ref[h], ds_ref[side])
        return carry

    lax.fori_loop(0, pairs, local, 0)
    for pair in range(pairs):
        dq_ref[pair] = (
            jnp.concatenate([dqt_ref[2 * pair], dqt_ref[2 * pair + 1]], axis=0) * (1.0 / LOG2E)
        ).T
    for apart, offset, count in slots:
        copies[apart].wait_recv()
        for tile in range(heads):
            dkv_ref[tile, :count, :] += rg_ref[tile, offset : offset + count, :].astype(f32)
    for pair in range(pairs):
        dkv_ref[pair] = dkv_ref[pair] * FACTOR
    from_heads([(dq_ref, pair) for pair in range(pairs)], base, d_ref.at[0], block)
    from_heads([(dkv_ref.at[:pairs], pair) for pair in range(pairs)], base, d_ref.at[1], block)
    from_heads([(dkv_ref.at[pairs:], pair) for pair in range(pairs)], base, d_ref.at[2], block)
    unspread = unspreader(heads * HD)

    def natural(t, carry):
        here = pl.ds(pl.multiple_of(t * CHUNK, CHUNK), CHUNK)
        for c in range(3):
            rows_here = dot(swap, d_ref[c, here, :]).astype(bf16)
            dmixed_ref[c, here, :] = dot(rows_here, unspread).astype(bf16)
        return carry

    lax.fori_loop(0, rows // CHUNK, natural, 0)
    for apart, _, _ in slots:
        copies[apart].wait_send()


def shape(dims, dtype):
    return jax.ShapeDtypeStruct(dims, dtype)


def project(tokens, aux, gain, w_qkv, heads):
    rows, width = tokens.shape
    return pl.pallas_call(
        partial(project_kernel, heads),
        out_shape=(
            shape((rows, width), bf16),
            shape((heads, rows, 128), bf16),
            shape((heads, rows, 128), bf16),
        ),
        in_specs=[VMEM] * 4,
        out_specs=(VMEM,) * 3,
        scratch_shapes=[pltpu.VMEM((rows, 3 * heads * SLOT), bf16)],
        compiler_params=pltpu.CompilerParams(vmem_limit_bytes=LIMIT),
    )(tokens, aux, gain.reshape(1, -1), w_qkv)


def attend(qz, kv, levels):
    heads, rows, _ = kv.shape
    half = rows // 2
    peers = (1 << levels) - 1
    return pl.pallas_call(
        partial(attend_kernel, levels, heads),
        out_shape=(
            shape((rows, heads * HD), bf16),
            shape((heads, SLOT, rows), f32),
            shape((heads, 1, rows), f32),
            shape((heads, levels * half, 128), bf16),
        ),
        in_specs=[VMEM] * 2,
        out_specs=(VMEM,) * 4,
        scratch_shapes=[
            pltpu.VMEM((heads, SLOT, rows), bf16),
            pltpu.VMEM((2, rows, half), f32),
            pltpu.VMEM((2, rows, half), bf16),
            pltpu.VMEM((heads, SLOT, rows), f32),
            pltpu.VMEM((heads, 1, rows), f32),
            pltpu.VMEM((heads // 2, rows, 128), f32),
            pltpu.VMEM((rows, heads * SLOT), bf16),
            pltpu.SemaphoreType.DMA((peers,)),
            pltpu.SemaphoreType.DMA((peers,)),
        ],
        compiler_params=pltpu.CompilerParams(
            vmem_limit_bytes=LIMIT, collective_id=0, has_side_effects=True
        ),
    )(qz, kv)


def attend_back(qz, kv, rk, d_attn, attn_t, bound, levels):
    heads, rows, _ = kv.shape
    half = rows // 2
    peers = (1 << levels) - 1
    return pl.pallas_call(
        partial(attend_back_kernel, levels, heads),
        out_shape=shape((3, rows, heads * HD), bf16),
        in_specs=[VMEM] * 6,
        out_specs=VMEM,
        scratch_shapes=[
            pltpu.VMEM((rows, heads * SLOT), bf16),
            pltpu.VMEM((heads, rows, 128), bf16),
            pltpu.VMEM((heads, 1, rows), f32),
            pltpu.VMEM((heads, SLOT, rows), bf16),
            pltpu.VMEM((2, rows, half), bf16),
            pltpu.VMEM((2, rows, half), bf16),
            pltpu.VMEM((heads, rows, 128), f32),
            pltpu.VMEM((heads, SLOT, rows), f32),
            pltpu.VMEM((heads // 2, rows, 128), f32),
            pltpu.VMEM((heads, levels * half, 128), bf16),
            pltpu.VMEM((heads, levels * half, 128), bf16),
            pltpu.VMEM((3, rows, heads * SLOT), bf16),
            pltpu.SemaphoreType.DMA((peers,)),
            pltpu.SemaphoreType.DMA((peers,)),
        ],
        compiler_params=pltpu.CompilerParams(
            vmem_limit_bytes=LIMIT, collective_id=1, has_side_effects=True
        ),
    )(qz, kv, rk, d_attn, attn_t, bound)


def normalize(rows_in, gain):
    centre = rows_in - jnp.mean(rows_in, axis=-1, keepdims=True)
    spread = jnp.mean(centre * centre, axis=-1, keepdims=True)
    return centre * lax.rsqrt(spread + EPS) * gain


def mask_columns(slide_ids, valid, wide):
    lane = jnp.arange(2 * wide, dtype=jnp.int32)[None, :]
    kind = lane % SLOT - HD
    slide, real = slide_ids[:, None], valid[:, None]
    query = ((kind >= 0) & (kind < 8) & (kind != slide)) | ((kind == 8) & (real == 1))
    key = ((kind >= 0) & (kind < 8) & (kind == slide)) | ((kind == 8) & (real == 0))
    return jnp.where(
        lane < wide, jnp.where(query, NEG, 0.0), jnp.where(key, 1.0, 0.0)
    ).astype(bf16)


def body(tokens, slide_ids, valid, norm_one, w_qkv, w_out, norm_two, w_up, w_down, cotangent):
    heads = w_out.shape[0] // HD
    levels = level_count(lax.axis_size("seq"))
    first = tokens.astype(f32)
    aux = mask_columns(slide_ids, valid, heads * SLOT)
    normed_low, qz, kv = project(tokens, aux, norm_one, w_qkv, heads)
    attn_low, attn_t, bound, rk = attend(qz, kv, levels)
    attn_term = jnp.dot(attn_low, w_out, preferred_element_type=f32)
    middle = first + lax.psum(attn_term.astype(bf16), "head").astype(f32)
    second, pull_two = jax.vjp(normalize, middle, norm_two)
    second_low = second.astype(bf16)
    up_proj = jnp.dot(second_low, w_up, preferred_element_type=f32)
    hidden, pull_gelu = jax.vjp(partial(jax.nn.gelu, approximate=False), up_proj)
    hidden_low = hidden.astype(bf16)
    mlp_term = jnp.dot(hidden_low, w_down, preferred_element_type=f32)
    output = (middle + lax.psum(mlp_term.astype(bf16), "head").astype(f32)).astype(bf16)
    grad_down = jnp.einsum("tf,td->fd", hidden_low, cotangent, preferred_element_type=f32)
    d_hidden = jnp.einsum("td,fd->tf", cotangent, w_down, preferred_element_type=f32)
    d_up = pull_gelu(d_hidden)[0].astype(bf16)
    grad_up = jnp.einsum("td,tf->df", second_low, d_up, preferred_element_type=f32)
    d_second_term = jnp.einsum("tf,df->td", d_up, w_up, preferred_element_type=f32)
    d_second = lax.psum(d_second_term.astype(bf16), "head").astype(f32)
    d_middle_norm, grad_norm_two = pull_two(d_second)
    d_middle = cotangent.astype(f32) + d_middle_norm
    d_branch = d_middle.astype(bf16)
    grad_out = jnp.einsum("te,td->ed", attn_low, d_branch, preferred_element_type=f32)
    d_attn = jnp.einsum("td,ed->te", d_branch, w_out, preferred_element_type=f32).astype(bf16)
    early = lax.psum(tuple(g.astype(bf16) for g in (grad_out, grad_up, grad_down)), "seq")
    d_mixed = attend_back(qz, kv, rk, d_attn, attn_t, bound, levels)
    grad_qkv = jnp.einsum("td,cte->cde", normed_low, d_mixed, preferred_element_type=f32)
    d_normed_term = jnp.einsum("cte,cde->td", d_mixed, w_qkv, preferred_element_type=f32)
    d_normed = lax.psum(d_normed_term.astype(bf16), "head").astype(f32)
    pull_one = jax.vjp(normalize, first, norm_one)[1]
    d_first, grad_norm_one = pull_one(d_normed)
    input_grad = d_middle + d_first
    norms = lax.psum(jnp.stack([grad_norm_one, grad_norm_two]), "seq")
    late = lax.psum(grad_qkv.astype(bf16), "seq")
    return (
        output, input_grad, norms[0], late.astype(f32), early[0].astype(f32), norms[1],
        early[1].astype(f32), early[2].astype(f32),
    )


def solution(mesh):
    placed = (
        P("seq", None), P("seq"), P("seq"), P(), P(None, None, "head"), P("head", None), P(),
        P(None, "head"), P("head", None), P("seq", None),
    )
    return jax.shard_map(
        body,
        mesh=mesh,
        in_specs=placed,
        out_specs=(
            P("seq", None), P("seq", None), P(), P(None, None, "head"), P("head", None), P(),
            P(None, "head"), P("head", None),
        ),
        check_vma=False,
    )
```

time: 958 us -> 468 us (0.49)
  local copies, waits for them, and re-layouts: 294 us -> 11.1 us
  other arithmetic: 142 us -> 35.3 us
  Pallas kernels: 0 us -> 95.7 us
  matrix products: 129 us -> 33.7 us
  waiting for transfers between devices: 320 us -> 247 us
  starting transfers between devices: 18.1 us -> 0.34 us
    broadcast_in_dim x83 -> x0, local copies, waits for them, and re-layouts: 147 us -> none  [the longest x56 117 us: place_rows(): spread_out = jnp.where(chosen, picked[:, None], fill)]
    pallas_call x0 -> x3, Pallas kernels: none -> 95.7 us  [the longest x1 45 us: attend_back(): pl.pallas_call(partial(attend_back_kernel, levels, heads), out_shape=shap...]
    dot_general x41 -> x11, matrix products: 128 us -> 33.7 us  [the longest x1 9.37 us: body(): jnp.einsum('td,fd->tf', cotangent, w_down, preferred_element_type=f32)]
    reduce_sum x30 -> x2, other arithmetic: 68.3 us -> 6.2 us  [normalize(): return centre * lax.rsqrt(spread + EPS) * gain]
    psum x4, waiting for transfers between devices: 296 us -> 247 us  [the longest x1 109 us: body(): late = lax.psum(grad_qkv.astype(bf16), 'seq')]
    unnamed x433 -> x55, local copies, waits for them, and re-layouts: 35.5 us -> 8.24 us
    ppermute x9 -> x0, waiting for transfers between devices: 24.3 us -> none  [partner(): return lax.ppermute(block, axis, route)]
    mul x13 -> x0, local copies, waits for them, and re-layouts: 19.6 us -> none  [the longest x8 13.8 us: body(): parts[which] * jnp.exp(totals[which] - bound)[:, :, None]]
  transfers between devices with their start and end apart: 13 -> 4, of which waited for: 8 -> 4; matrix products, arithmetic and copies ran while one was open for 34% -> 6% of each run, Pallas kernels for 0% -> 0%
where the time goes in v1:
time: 468 us; the launch traced here: 461 us
  waiting for transfers between devices  247 us (53%)
  Pallas kernels  95.7 us (20%)
  other arithmetic  35.3 us (8%)
  matrix products  33.7 us (7%)
  blocking collectives  23 us (5%)
  between operations  14.6 us (3%)
  local copies, waits for them, and re-layouts  11.1 us (2%)
    psum x1, waiting for transfers between devices, body(): late = lax.psum(grad_qkv.astype(bf16), 'seq')  109 us
    psum x1, waiting for transfers between devices, body(): lax.psum(mlp_term.astype(bf16), 'head').astype(f32)  58.6 us
    pallas_call x1, Pallas kernels, attend_back(): pl.pallas_call(partial(attend_back_kernel, levels, heads), out_shape=shap...  45 us
    psum x1, waiting for transfers between devices, body(): middle = first + lax.psum(attn_term.astype(bf16), 'head').astype(f32)  43.3 us
    pallas_call x1, Pallas kernels, attend(): pl.pallas_call(partial(attend_kernel, levels, heads), out_shape=(shape((r...  39.2 us
    psum x1, waiting for transfers between devices, body(): d_second = lax.psum(d_second_term.astype(bf16), 'head').astype(f32)  36 us
    psum x1, blocking collectives, body(): norms = lax.psum(jnp.stack([grad_norm_one, grad_norm_two]), 'seq')  23 us
    pallas_call x1, Pallas kernels, project(): pl.pallas_call(partial(project_kernel, heads), out_shape=(shape((rows, wi...  11.6 us
  transfers between devices with their start and end apart: 4, of which 4 were waited for; matrix products, arithmetic and copies ran while one was open for 6% of the time, Pallas kernels for 0%

profile of v1, /device:TPU:0, one launch (start us, length us, event | category | flops | bytes accessed | tf_op | source)
XLA Modules:
  0.0 461.0 jit_solution(13590572325980691941)
XLA Ops:
  8.0 1.3 reshape.116.gain_ref
  9.3 2.3 copy.22.w_ref
  11.6 2.8 select_convert_fusion.aux_ref
  14.4 11.6 %shard_map.161 = (bf16[1024,768]{1,0:T(8,128)(2,1)}, bf16[4,1024,128]{2,1,0:T(8,128)(2,1)}, bf16[4,1024,128]{2,1,0:T(8,128)(2,1)}) custom-call(bf16[1024,768]{1,0:T(8,128)(2,1)} %tokens_ref.1, bf16[1024,512]{1,0:T(8,128)(2,1)} %select_convert_fusion.aux_ref, f32[1,768]{1,0:T(1,128)} %reshape.116.gain_ref, bf16[3,768,192]{2,1,0:T(8,128)(2,1)} %copy.22.w_ref), custom_call_target="tpu_custom_call" | custom-call | tf_op jit(solution)/shard_map/pallas_call | solution.py:421
  26.0 39.2 %shard_map.162 = (bf16[1024,192]{1,0:T(8,128)(2,1)}, f32[4,64,1024]{2,1,0:T(8,128)}, f32[4,1,1024]{2,1,0:T(1,128)}, bf16[4,1536,128]{2,1,0:T(8,128)(2,1)}) custom-call(bf16[4,1024,128]{2,1,0:T(8,128)(2,1)} %get-tuple-element.15.qz_ref, bf16[4,1024,128]{2,1,0:T(8,128)(2,1)} %get-tuple-element.16.kv_ref), custom_call_target="tpu_custom_call" | custom-call | tf_op jit(solution)/shard_map/pallas_call | solution.py:439
  65.2 2.7 convolution_convert_fusion.2
  68.2 43.3 %all-reduce.7.cloned.1.call-done = bf16[1024,768]{1,0:T(8,128)(2,1)} async-done(((bf16[1024,768]{1,0:T(8,128)(2,1)}), bf16[1024,768]{1,0:T(8,128)(2,1)}) %all-reduce.7.cloned.1.call-update) | async-done | bytes 1572880 | tf_op jit(solution)/shard_map/psum | solution.py:522
  111.5 2.0 fusion.19
  115.6 1.4 fusion.38
  117.6 9.4 %add_convert_fusion = (bf16[1024,768]{1,0:T(8,128)(2,1)S(1)}, f32[1024,768]{1,0:T(8,128)}) fusion(f32[1024,768]{1,0:T(8,128)S(1)} %fusion.38, bf16[1024,768]{1,0:T(8,128)(2,1)S(1)} %copy-done.6, bf16[768,768]{1,0:T(8,128)(2,1)S(1)} %copy-done), kind=kOutput, calls=%fused_computation.26 | convolution fusion | flops 1264582656 | bytes 10616832 | tf_op jit(solution)/shard_map/td,fd->tf/dot_general | solution.py:531
  128.2 2.6 convolution_convert_fusion
  130.8 3.3 multiply_convert_fusion
  135.3 2.5 convolution_convert_fusion.1
  137.8 36.0 %all-reduce.9.cloned.1.call-done = bf16[1024,768]{1,0:T(8,128)(2,1)} async-done(((bf16[1024,768]{1,0:T(8,128)(2,1)}), bf16[1024,768]{1,0:T(8,128)(2,1)}) %all-reduce.9.cloned.1.call-update) | async-done | bytes 1572880 | tf_op jit(solution)/shard_map/psum | solution.py:535
  173.8 4.2 fusion.8
  178.1 1.7 fusion.36
  184.3 45.0 %shard_map.163 = bf16[3,1024,192]{2,1,0:T(8,128)(2,1)} custom-call(bf16[4,1024,128]{2,1,0:T(8,128)(2,1)} %get-tuple-element.15.qz_ref, bf16[4,1024,128]{2,1,0:T(8,128)(2,1)} %get-tuple-element.16.kv_ref, bf16[4,1536,128]{2,1,0:T(8,128)(2,1)} %get-tuple-element.18.rk_ref, bf16[1024,192]{1,0:T(8,128)(2,1)} %copy.23.da_ref, ...), custom_call_target="tpu_custom_call" | custom-call | tf_op jit(solution)/shard_map/pallas_call | solution.py:470
  229.3 4.0 bitcast_convert_fusion
  233.4 4.6 convolution_convert_fusion.4
  238.0 2.5 convolution_convert_fusion.3
  240.5 1.2 convolution_convert_fusion.6
  241.7 2.1 fusion.27
  243.9 58.6 %all-reduce.13.cloned.1.call-done = (bf16[1024,768]{1,0:T(8,128)(2,1)}, bf16[1024,768]{1,0:T(8,128)(2,1)}) async-done(((bf16[1024,768]{1,0:T(8,128)(2,1)}, bf16[1024,768]{1,0:T(8,128)(2,1)}), (bf16[1024,768]{1,0:T(8,128)(2,1)}, bf16[1024,768]{1,0:T(8,128)(2,1)})) %all-reduce.13.cloned.1.call-update) | async-done | bytes 3145744 | tf_op jit(solution)/shard_map/psum | solution.py:529
  302.5 2.7 fusion.10
  305.2 2.0 fusion.9
  307.2 23.0 %psum.67 = f32[2,768]{1,0:T(2,128)S(1)} all-reduce(f32[2,768]{1,0:T(2,128)S(1)} %pad_maximum_fusion), channel_id=1, replica_groups=mesh['seq'=8,'head'=4] {'seq'}, use_global_device_ids=true, to_apply=%region_14.15 | all-reduce | flops 1536 | bytes 12288 | tf_op jit(solution)/shard_map/psum | solution.py:549
  330.9 6.1 %add_add_fusion.2 = (f32[1024,768]{1,0:T(8,128)}, bf16[1024,768]{1,0:T(8,128)(2,1)}) fusion(bf16[1024,768]{1,0:T(8,128)(2,1)S(1)} %copy-done.1, bf16[1024,768]{1,0:T(8,128)(2,1)} %get-tuple-element.36, f32[1024,768]{1,0:T(8,128)} %copy-done.4, bf16[1024,768]{1,0:T(8,128)(2,1)} %param.19, f32[1024]{0:T(1024)S(1)} %negate_multiply_fusion.1, ...), kind=kLoop, calls=%fused_computation.24 | loop fusion | flops 14155776 | bytes 15752192 | tf_op jit(solution)/shard_map/add | solution.py:548
  337.0 109.4 %all-reduce.11.cloned.1.call-done = (bf16[3,768,192]{1,2,0:T(8,128)(2,1)}, bf16[192,768]{1,0:T(8,128)(2,1)}, bf16[768,768]{1,0:T(8,128)(2,1)}, bf16[768,768]{1,0:T(8,128)(2,1)}) async-done(((bf16[3,768,192]{1,2,0:T(8,128)(2,1)}, bf16[192,768]{1,0:T(8,128)(2,1)}, bf16[768,768]{1,0:T(8,128)(2,1)}, bf16[768,768]{1,0:T(8,128)(2,1)}), (bf16[3,768,192]{1,2,0:T(8,128)(2,1)}, bf16[192,768]{1,0:T(8,128)(2,1)}, ...) | async-done | bytes 3538960 | tf_op jit(solution)/shard_map/psum | solution.py:550
  446.3 1.9 convert_element_type.99
  448.2 2.6 convert_element_type.97
  450.9 1.6 convert_element_type.101
  452.4 1.6 convert_element_type.103
  (82 shorter events, 11.4 us)
Async XLA Ops:
  7.2 109.8 %copy-start = (bf16[768,768]{1,0:T(8,128)(2,1)S(1)}, bf16[768,768]{1,0:T(8,128)(2,1)}, u32[]{:S(2)}) copy-start(bf16[768,768]{1,0:T(8,128)(2,1)} %param.18) | copy-start | bytes 3538948
  7.2 104.3 %all-reduce.7.cloned.1.call-start = ((), (), s32[]{:S(2)}) async-start(), calls=%async_computation | async-start | bytes 3145728 | tf_op jit(solution)/shard_map/psum | solution.py:522
  14.4 50.7 %copy-start.21 = (bf16[192,768]{1,0:T(8,128)(2,1)S(1)}, bf16[192,768]{1,0:T(8,128)(2,1)}, u32[]{:S(2)}) copy-start(bf16[192,768]{1,0:T(8,128)(2,1)} %param.15) | copy-start | bytes 884740
  26.0 85.5 %copy-start.1 = (bf16[1024,768]{1,0:T(8,128)(2,1)S(1)}, bf16[1024,768]{1,0:T(8,128)(2,1)}, u32[]{:S(2)}) copy-start(bf16[1024,768]{1,0:T(8,128)(2,1)} %tokens_ref.1) | copy-start | bytes 4718596
  68.0 46.4 %copy-start.23 = (f32[768]{0:T(1024)S(1)}, f32[768]{0:T(1024)}, u32[]{:S(2)}) copy-start(f32[768]{0:T(1024)} %param.16) | copy-start | bytes 9220
  68.0 105.9 %all-reduce.9.cloned.1.call-start = ((), (), s32[]{:S(2)}) async-start(), calls=%async_computation.1 | async-start | bytes 3145728 | tf_op jit(solution)/shard_map/psum | solution.py:535
  111.5 2.0 copy-start.2
  114.3 1.3 copy-start.25
  115.6 1.4 copy-start.11
  115.6 2.0 copy-start.6
  117.6 9.4 %copy-start.10 = (f32[1024,768]{1,0:T(8,128)}, f32[1024,768]{1,0:T(8,128)S(1)}, u32[]{:S(2)}) copy-start(f32[1024,768]{1,0:T(8,128)S(1)} %fusion.38) | copy-start | bytes 9437188
  127.0 1.2 copy-start.26
  130.8 171.7 %all-reduce.13.cloned.1.call-start = ((), (), s32[]{:S(2)}) async-start(), calls=%async_computation.3 | async-start | bytes 6291456 | tf_op jit(solution)/shard_map/psum | solution.py:529
  134.1 1.2 copy-start.14
  173.8 4.3 copy-start.3
  173.8 4.3 copy-start.9
  178.1 1.7 copy-start.7
  179.8 1.7 copy-start.4
  181.5 1.1 copy-start.12
  184.3 45.0 %copy-start.19 = (bf16[3,768,192]{1,2,0:T(8,128)(2,1)S(1)}, bf16[3,768,192]{1,2,0:T(8,128)(2,1)}, u32[]{:S(2)}) copy-start(bf16[3,768,192]{1,2,0:T(8,128)(2,1)} %param.14) | copy-start | bytes 2654212
  233.3 213.0 %all-reduce.11.cloned.1.call-start = ((), (), s32[]{:S(2)}) async-start(), calls=%async_computation.2 | async-start | bytes 7077888 | tf_op jit(solution)/shard_map/psum | solution.py:550
  233.4 4.6 copy-start.8
  233.4 4.6 copy-start.15
  237.9 2.5 copy-start.13
  238.0 2.5 copy-start.20
  238.0 3.7 copy-start.16
  238.0 3.7 copy-start.24
  243.8 58.7 %copy-start.22 = (f32[768]{0:T(1024)S(1)}, f32[768]{0:T(1024)}, u32[]{:S(2)}) copy-start(f32[768]{0:T(1024)} %param.13) | copy-start | bytes 9220
  302.5 2.7 copy-start.5
  446.3 4.5 copy-start.18
  448.2 4.2 copy-start.17
Sparse Core Ops, SparseCore 0:
  68.1 43.3 all-reduce.6
  130.9 42.9 all-reduce.8
  233.4 69.0 all-reduce.12
  306.9 139.3 all-reduce.10

commit v2 on v1

--- a/solution.py
+++ b/solution.py
@@ -27,6 +27,10 @@
     return jnp.dot(a, b, preferred_element_type=f32)
 
 
+def dot_tn(a, b):
+    return lax.dot_general(a, b, (((0,), (0,)), ((), ())), preferred_element_type=f32)
+
+
 def dot_nt(a, b):
     return lax.dot_general(a, b, NT, preferred_element_type=f32)
 
@@ -99,11 +103,157 @@
     return jnp.minimum(key, query) + (1.0 if level is None else -1.0 * level)
 
 
-def greet(peers, axis):
+def greet(peers):
     barrier = pltpu.get_barrier_semaphore()
-    for peer in peers:
+    for axis, peer in peers:
         pl.semaphore_signal(barrier, inc=1, device_id={axis: peer}, device_id_type=MESH)
     pl.semaphore_wait(barrier, len(peers))
+
+
+def seq_sum(me, src, out, buf, sem, slot, order):
+    lo, size, offset, halved, sent = 0, src.shape[0], 0, [], []
+    halvings = min(2, len(order) - 1)
+    for step, bit in enumerate(order):
+        mine = me // (1 << bit) % 2
+        peer = peer_of(me, 1 << bit)
+        if step < halvings:
+            size = size // 2
+            give = pl.multiple_of(lo + (1 - mine) * size, 16)
+            halved.append((bit, mine, lo))
+            lo = pl.multiple_of(lo + mine * size, 16)
+        else:
+            give = lo
+        here = pl.ds(lo, size)
+        landed = slice(offset, offset + size)
+        copy = remote(src.at[pl.ds(give, size)], buf.at[landed], sem, (slot, step), "seq", peer)
+        copy.start()
+        yield
+        copy.wait_recv()
+        if step < halvings:
+            sent.append(copy)
+        elif step < len(order) - 1:
+            copy.wait_send()
+        else:
+            sent.append(copy)
+        value = (src[here].astype(f32) + buf[landed].astype(f32)).astype(bf16)
+        if step < len(order) - 1:
+            src[here] = value
+        else:
+            out[here] = value
+        offset += size
+    for step, (bit, mine, before) in enumerate(reversed(halved)):
+        here = out.at[pl.ds(lo, size)]
+        copy = remote(here, here, sem, (slot, len(order) + step), "seq", peer_of(me, 1 << bit))
+        copy.start()
+        yield
+        copy.wait_recv()
+        sent.append(copy)
+        lo, size = before, size * 2
+    for copy in sent:
+        copy.wait_send()
+
+
+def gain_sum(all_bits, mine, got, sem):
+    sent = []
+    for step, (axis, bit) in enumerate(all_bits):
+        peer = peer_of(lax.axis_index(axis), 1 << bit)
+        copy = remote(mine.at[step], got.at[step], sem, (step,), axis, peer)
+        copy.start()
+        yield
+        copy.wait_recv()
+        sent.append(copy)
+        mine[step + 1] = mine[step] + got[step]
+    for copy in sent:
+        copy.wait_send()
+
+
+def pump(*jobs):
+    for job in jobs:
+        next(job, None)
+
+
+def remote(src, dst, sem, index, axis, peer):
+    return pltpu.make_async_remote_copy(
+        src_ref=src,
+        dst_ref=dst,
+        send_sem=sem.at[(0,) + index],
+        recv_sem=sem.at[(1,) + index],
+        device_id={axis: peer},
+        device_id_type=MESH,
+    )
+
+
+class Place:
+    def __init__(self):
+        self.me = lax.axis_index("head")
+        self.core, self.side = self.me % 2, self.me // 2
+        self.partner = self.me + 1 - 2 * self.core
+        self.across = self.me + 2 - 4 * self.side
+
+    def peers(self):
+        return [("head", self.partner), ("head", self.across)]
+
+
+class HeadSum:
+    def __init__(self, place, term, got, half, last, sem, slot):
+        self.place, self.term, self.got, self.half, self.last = place, term, got, half, last
+        self.sem, self.slot = sem, slot
+
+    def near(self, s):
+        src = self.term.at[s, 1 - self.place.core]
+        return remote(src, self.got.at[s], self.sem, (self.slot, s), "head", self.place.partner)
+
+    def far(self, s):
+        return remote(
+            self.half.at[s], self.last.at[s], self.sem, (self.slot + 1, s), "head", self.place.across
+        )
+
+    def start(self, s):
+        self.near(s).start()
+
+    def forward(self, s):
+        self.near(s).wait_recv()
+        core, other = self.place.core, 1 - self.place.side
+        both = self.term[s, core, other].astype(f32) + self.got[s, other].astype(f32)
+        self.half[s] = both.astype(bf16)
+        self.far(s).start()
+
+    def total(self, s):
+        self.far(s).wait_recv()
+        core, side = self.place.core, self.place.side
+        both = self.term[s, core, side].astype(f32) + self.got[s, side].astype(f32)
+        return both + self.last[s].astype(f32)
+
+    def finish(self, s):
+        self.near(s).wait_send()
+        self.far(s).wait_send()
+
+
+class HeadSpread:
+    def __init__(self, place, at, sem, slot):
+        self.place, self.at, self.sem, self.slot = place, at, sem, slot
+
+    def copy(self, s, kind):
+        place = self.place
+        ref = self.at(place.core, 1 - place.side if kind == 2 else place.side, s)
+        peer = place.across if kind == 0 else place.partner
+        return remote(ref, ref, self.sem, (self.slot + kind, s), "head", peer)
+
+    def start(self, s):
+        self.copy(s, 0).start()
+        self.copy(s, 1).start()
+
+    def relay(self, s):
+        self.copy(s, 0).wait_recv()
+        self.copy(s, 2).start()
+
+    def arrive(self, s):
+        self.copy(s, 1).wait_recv()
+        self.copy(s, 2).wait_recv()
+
+    def finish(self, s):
+        for kind in range(3):
+            self.copy(s, kind).wait_send()
 
 
 def half_mask(which, rows):
@@ -158,7 +308,7 @@
         normed = (centre * lax.rsqrt(spread_of + EPS) * gain_ref[...]).astype(bf16)
         normed_ref[here, :] = normed
         for c in range(3):
-            y = dot(normed, w_ref[c])
+            y = dot_nt(normed, w_ref[c])
             if c == 1:
                 y = y * (FACTOR * LOG2E)
             y = dot(y.astype(bf16), spread)
@@ -208,7 +358,7 @@
     block = rows // CLASSES
     me = lax.axis_index("seq")
     slots = [slot for level in range(levels) for slot in slots_of(level, half)]
-    greet([peer_of(me, apart) for apart, _, _ in slots], "seq")
+    greet([("seq", peer_of(me, apart)) for apart, _, _ in slots])
     copies = {}
     for apart, offset, count in slots:
         copies[apart] = pltpu.make_async_remote_copy(
@@ -284,22 +434,217 @@
         copies[apart].wait_send()
 
 
-def attend_back_kernel(
-    levels, heads, qz_ref, kv_ref, rk_ref, da_ref, attn_t_ref, bound_ref, dmixed_ref,
+def unit_rows(rows_in):
+    centre = rows_in - jnp.mean(rows_in, axis=-1, keepdims=True)
+    spread = jnp.mean(centre * centre, axis=-1, keepdims=True)
+    scale = lax.rsqrt(spread + EPS)
+    return centre * scale, scale
+
+
+def norm_back(grad, gain, unit, scale):
+    n = grad * gain
+    shift = jnp.mean(n, axis=-1, keepdims=True)
+    along = jnp.mean(n * unit, axis=-1, keepdims=True)
+    return scale * (n - shift - unit * along)
+
+
+PARTS = 4
+
+
+def middle_kernel(
+    attn_ref, w_out_ref, tokens_ref, gain_ref, w_up_ref, w_down_ref, cot_ref,
+    d_attn_ref, middle_ref, d_middle_ref, mlp_ref, grad_out_ref, grad_up_ref, grad_down_ref, gain_grad_ref,
+    a_ref, hidden_ref, d_hidden_ref, d_up_ref, second_ref, branch_ref,
+    term_ref, got_ref, half_ref, last_ref, back_ref, back_got_ref, back_half_ref, back_last_ref, sem,
+):
+    own, width = middle_ref.shape
+    sub = own // PARTS
+    chunk = 4 * sub
+    units = w_up_ref.shape[1]
+    tile = 256
+    place = Place()
+    greet(place.peers())
+    gain = gain_ref[...]
+    forth = HeadSum(place, term_ref, got_ref, half_ref, last_ref, sem, 0)
+    back = HeadSum(place, back_ref, back_got_ref, back_half_ref, back_last_ref, sem, 2)
+    seconds = HeadSpread(place, lambda core, side, s: second_ref.at[s, core, side], sem, 4)
+    branches = HeadSpread(place, lambda core, side, s: branch_ref.at[s, core, side], sem, 7)
+
+    def rows_of(s, k):
+        return pl.ds(pl.multiple_of((2 * (k % 2) + k // 2) * own + s * sub, sub), sub)
+
+    def mine_of(s):
+        return pl.ds(pl.multiple_of(place.me * own + s * sub, sub), sub)
+
+    def owned(s):
+        return pl.ds(pl.multiple_of(s * sub, sub), sub)
+
+    def chunk_of(s):
+        return pl.ds(pl.multiple_of(s * chunk, chunk), chunk)
+
+    def gather(ref, s):
+        return jnp.concatenate([ref[rows_of(s, k), :] for k in range(4)], axis=0)
+
+    def split(ref, s, value):
+        for k in range(4):
+            ref[s, k // 2, k % 2] = value[k * sub : k * sub + sub]
+
+    def joined(ref, s):
+        return jnp.concatenate([ref[s, k // 2, k % 2] for k in range(4)], axis=0)
+
+    def each(step):
+        def run(s, carry):
+            step(s)
+            return carry
+
+        lax.fori_loop(0, PARTS, run, 0)
+
+    def project_out(s):
+        a = gather(attn_ref, s)
+        a_ref[chunk_of(s), :] = a
+        split(term_ref, s, dot(a, w_out_ref[...]).astype(bf16))
+        forth.start(s)
+
+    def hidden_back(s):
+        d_hidden_ref[chunk_of(s), :] = dot_nt(gather(cot_ref, s), w_down_ref[...])
+
+    def norm_rows(s):
+        rows = tokens_ref[mine_of(s), :].astype(f32) + forth.total(s)
+        middle_ref[owned(s), :] = rows
+        unit, _ = unit_rows(rows)
+        second_ref[s, place.core, place.side] = (unit * gain).astype(bf16)
+        seconds.start(s)
+
+    def feed(s):
+        second = joined(second_ref, s)
+        for j in range(0, units, tile):
+            lanes = slice(j, j + tile)
+            up = dot(second, w_up_ref[:, lanes])
+            cdf = 0.5 + 0.5 * lax.erf(up * (0.5**0.5))
+            hidden = (up * cdf).astype(bf16)
+            slope = cdf + up * jnp.exp2(up * up * (-0.5 * LOG2E)) * 0.3989422804014327
+            for k in range(4):
+                hidden_ref[rows_of(s, k), lanes] = hidden[k * sub : k * sub + sub]
+            d_up_ref[chunk_of(s), lanes] = (d_hidden_ref[chunk_of(s), lanes] * slope).astype(bf16)
+
+    def feed_sums(s):
+        split(back_ref, s, dot_nt(d_up_ref[chunk_of(s), :], w_up_ref[...]).astype(bf16))
+        back.start(s)
+        down = dot(gather(hidden_ref, s), w_down_ref[...]).astype(bf16)
+        for k in range(4):
+            mlp_ref[0, k // 2, k % 2, owned(s), :] = down[k * sub : k * sub + sub]
+
+    def norm_rows_back(s):
+        grad = back.total(s)
+        unit, scale = unit_rows(middle_ref[owned(s), :])
+        gain_grad_ref[...] += jnp.sum(grad * unit, axis=0, keepdims=True)
+        d_middle = cot_ref[mine_of(s), :].astype(f32) + norm_back(grad, gain, unit, scale)
+        d_middle_ref[owned(s), :] = d_middle
+        branch_ref[s, place.core, place.side] = d_middle.astype(bf16)
+        branches.start(s)
+
+    def attn_back(s):
+        branches.arrive(s)
+        d_attn = dot_nt(joined(branch_ref, s), w_out_ref[...]).astype(bf16)
+        for k in range(4):
+            d_attn_ref[rows_of(s, k), :] = d_attn[k * sub : k * sub + sub]
+
+    gain_grad_ref[...] = jnp.zeros_like(gain_grad_ref)
+    each(project_out)
+    each(hidden_back)
+    each(forth.forward)
+    each(norm_rows)
+    each(seconds.relay)
+
+    def tick(s, carry):
+        seconds.arrive(s)
+        feed(s)
+
+        @pl.when(s >= 1)
+        def _():
+            back.forward(s - 1)
+
+        @pl.when(s >= 2)
+        def _():
+            norm_rows_back(s - 2)
+
+        @pl.when(s >= 3)
+        def _():
+            branches.relay(s - 3)
+
+        feed_sums(s)
+        return carry
+
+    lax.fori_loop(0, PARTS, tick, 0)
+    back.forward(PARTS - 1)
+    norm_rows_back(PARTS - 2)
+    for j in range(0, units, tile):
+        grad_down_ref[j : j + tile, :] = dot_tn(hidden_ref[:, j : j + tile], cot_ref[...]).astype(bf16)
+    branches.relay(PARTS - 3)
+    norm_rows_back(PARTS - 1)
+    for j in range(0, width, tile):
+        second = second_ref[:, :, :, :, j : j + tile].reshape(PARTS * chunk, tile)
+        grad_up_ref[j : j + tile, :] = dot_tn(second, d_up_ref[...]).astype(bf16)
+    branches.relay(PARTS - 2)
+    branches.relay(PARTS - 1)
+    each(attn_back)
+    for j in range(0, width, tile):
+        branch = branch_ref[:, :, :, :, j : j + tile].reshape(PARTS * chunk, tile)
+        grad_out_ref[:, j : j + tile] = dot_tn(a_ref[...], branch).astype(bf16)
+    for mover in (forth, back, seconds, branches):
+        each(mover.finish)
+
+
+def back_kernel(
+    levels, heads, orders,
+    qz_ref, kv_ref, rk_ref, da_ref, attn_t_ref, bound_ref, middle_ref, d_middle_ref, mlp_ref,
+    part_out_ref, part_up_ref, part_down_ref, part_gain_ref, tokens_ref, gain_ref, normed_ref, w_ref,
+    output_ref, input_grad_ref, grad_out_ref, grad_up_ref, grad_down_ref, grad_qkv_ref, gains_ref,
     cls_ref, doz_ref, delta_ref, kt_ref, p_ref, ds_ref, dkv_ref, dqt_ref, dq_ref, sb_ref, rg_ref, d_ref,
-    send_sem, recv_sem,
+    dm_ref, mlp_got_ref, mlp_half_ref, mlp_last_ref, term_ref, got_ref, half_ref, last_ref,
+    src_out_ref, src_up_ref, src_down_ref, src_qkv_ref, buf_out_ref, buf_up_ref, buf_down_ref, buf_qkv_ref,
+    gain_mine_ref, gain_got_ref, send_sem, recv_sem, head_sem, part_sem, seq_sem, gain_sem,
 ):
     rows = kv_ref.shape[1]
     half = rows // 2
     block = rows // CLASSES
+    own = rows // 4
+    sub = own // PARTS
     pairs = heads // 2
     wide = heads * SLOT
+    width = heads * HD
     me = lax.axis_index("seq")
     base = lax.axis_index("head") * heads
+    place = Place()
     slots = [slot for level in range(levels) for slot in slots_of(level, half)]
-    greet([peer_of(me, apart) for apart, _, _ in slots], "seq")
+    apart_all = sorted({apart for apart, _, _ in slots} | {1 << bit for bit in orders[0]})
+    greet([("seq", peer_of(me, apart)) for apart in apart_all] + place.peers())
+
+    def mine_of(s, rows_each):
+        return pl.ds(pl.multiple_of(place.me * own + s * rows_each, rows_each), rows_each)
+
+    def natural_at(ref, rows_each):
+        def at(core, side, s):
+            start = (2 * side + core) * own + s * rows_each
+            return ref.at[pl.ds(pl.multiple_of(start, rows_each), rows_each), :]
+
+        return at
+
+    mlp_sum = HeadSum(place, mlp_ref, mlp_got_ref, mlp_half_ref, mlp_last_ref, head_sem, 0)
+    outputs = HeadSpread(place, natural_at(output_ref, own), head_sem, 2)
+    normed_sum = HeadSum(place, term_ref, got_ref, half_ref, last_ref, part_sem, 0)
+    inputs = HeadSpread(place, natural_at(input_grad_ref, sub), part_sem, 2)
+    src_up_ref[...] = part_up_ref[...]
+    src_down_ref[...] = part_down_ref[...]
+    src_out_ref[...] = part_out_ref[...]
+    ups = seq_sum(me, src_up_ref, grad_up_ref, buf_up_ref, seq_sem, 0, orders[0])
+    downs = seq_sum(me, src_down_ref, grad_down_ref, buf_down_ref, seq_sem, 1, orders[1])
+    outs = seq_sum(me, src_out_ref, grad_out_ref, buf_out_ref, seq_sem, 2, orders[0])
+    mlp_sum.start(0)
+    pump(ups, downs)
+
     swap = digit_swap()
-    spread = spreader(heads * HD)
+    spread = spreader(width)
     for t in range(rows // CHUNK):
         y = dot(da_ref[t * CHUNK : t * CHUNK + CHUNK, :], spread).astype(bf16)
         y = dot(swap, y).astype(bf16)
@@ -319,6 +664,7 @@
     for h in range(heads):
         turned = dot_nt(unit, doz_ref[h])[h % 2 * SLOT : h % 2 * SLOT + SLOT]
         delta_ref[h] = jnp.sum(turned * attn_t_ref[h], axis=0, keepdims=True)
+    mlp_sum.forward(0)
 
     dqt_ref[...] = jnp.zeros_like(dqt_ref)
     copies = {}
@@ -327,7 +673,7 @@
         keys = slice(level * half, level * half + half)
         transpose_heads(rk_ref, 0, level * half, half, kt_ref, heads)
 
-        def remote(pair, carry):
+        def remote_keys(pair, carry):
             counts = pair_counts(half, queries, half, level)
             dk = jnp.zeros((half, 128), f32)
             dv = jnp.zeros((half, 128), f32)
@@ -344,7 +690,7 @@
             sb_ref[pairs + pair, keys, :] = dv.astype(bf16)
             return carry
 
-        lax.fori_loop(0, pairs, remote, 0)
+        lax.fori_loop(0, pairs, remote_keys, 0)
         for apart, offset, count in slots_of(level, half):
             copies[apart] = pltpu.make_async_remote_copy(
                 src_ref=sb_ref.at[:, offset : offset + count, :],
@@ -356,6 +702,9 @@
             )
             copies[apart].start()
 
+    output_ref[mine_of(0, own), :] = (middle_ref[...] + mlp_sum.total(0)).astype(bf16)
+    outputs.start(0)
+    pump(ups, downs, outs)
     transpose_heads(kv_ref, 0, 0, rows, kt_ref, heads)
 
     def local(pair, carry):
@@ -384,7 +733,11 @@
                 dqt_ref[h, :, there] += dot(kt_ref[h], ds_ref[side])
         return carry
 
-    lax.fori_loop(0, pairs, local, 0)
+    for pair in range(pairs):
+        local(pair, 0)
+        if pair == 0:
+            outputs.relay(0)
+        pump(ups, downs, outs)
     for pair in range(pairs):
         dq_ref[pair] = (
             jnp.concatenate([dqt_ref[2 * pair], dqt_ref[2 * pair + 1]], axis=0) * (1.0 / LOG2E)
@@ -398,16 +751,68 @@
     from_heads([(dq_ref, pair) for pair in range(pairs)], base, d_ref.at[0], block)
     from_heads([(dkv_ref.at[:pairs], pair) for pair in range(pairs)], base, d_ref.at[1], block)
     from_heads([(dkv_ref.at[pairs:], pair) for pair in range(pairs)], base, d_ref.at[2], block)
-    unspread = unspreader(heads * HD)
-
-    def natural(t, carry):
-        here = pl.ds(pl.multiple_of(t * CHUNK, CHUNK), CHUNK)
+    unspread = unspreader(width)
+
+    def natural(k, carry):
+        core = (place.core + 1 + k // 2) % 2
+        side = k % 2
+        here = pl.ds(pl.multiple_of((2 * side + core) * CHUNK, CHUNK), CHUNK)
+        term = jnp.zeros((CHUNK, normed_ref.shape[1]), f32)
         for c in range(3):
             rows_here = dot(swap, d_ref[c, here, :]).astype(bf16)
-            dmixed_ref[c, here, :] = dot(rows_here, unspread).astype(bf16)
+            mixed = dot(rows_here, unspread).astype(bf16)
+            dm_ref[c, here, :] = mixed
+            term = term + dot(mixed, w_ref[c])
+        term = term.astype(bf16)
+        for s in range(PARTS):
+            term_ref[s, core, side] = term[s * sub : s * sub + sub]
         return carry
 
-    lax.fori_loop(0, rows // CHUNK, natural, 0)
+    def each(step):
+        def run(s, carry):
+            step(s)
+            return carry
+
+        lax.fori_loop(0, PARTS, run, 0)
+
+    lax.fori_loop(0, 2, natural, 0)
+    each(normed_sum.start)
+    lax.fori_loop(2, 4, natural, 0)
+    each(normed_sum.forward)
+    for c in range(3):
+        src_qkv_ref[c] = dot_tn(dm_ref[c], normed_ref[...]).astype(bf16)
+    qkvs = [
+        seq_sum(me, src_qkv_ref.at[c], grad_qkv_ref.at[c], buf_qkv_ref.at[c], seq_sem, 3 + c, orders[c % 2])
+        for c in range(3)
+    ]
+    pump(*qkvs)
+    gain = gain_ref[...]
+    gain_mine_ref[0] = jnp.zeros_like(gain_mine_ref[0])
+    gain_mine_ref[0, 1:2, :] = part_gain_ref[...]
+
+    def rows_back(s):
+        grad = normed_sum.total(s)
+        unit_in, scale = unit_rows(tokens_ref[mine_of(s, sub), :].astype(f32))
+        gain_mine_ref[0, 0:1, :] += jnp.sum(grad * unit_in, axis=0, keepdims=True)
+        here = pl.ds(pl.multiple_of(s * sub, sub), sub)
+        grad_in = d_middle_ref[here, :] + norm_back(grad, gain, unit_in, scale)
+        input_grad_ref[mine_of(s, sub), :] = grad_in.astype(bf16)
+        inputs.start(s)
+
+    each(rows_back)
+    bits = [("head", 0), ("head", 1)] + [("seq", bit) for bit in orders[0]]
+    gains = gain_sum(bits, gain_mine_ref, gain_got_ref, gain_sem)
+    pump(ups, downs, outs, gains, *qkvs)
+    each(inputs.relay)
+    for _ in range(2 * len(bits) + 4):
+        pump(gains, ups, downs, outs, *qkvs)
+    gains_ref[...] = gain_mine_ref[len(bits)]
+    each(inputs.arrive)
+    outputs.arrive(0)
+    each(normed_sum.finish)
+    each(inputs.finish)
+    mlp_sum.finish(0)
+    outputs.finish(0)
     for apart, _, _ in slots:
         copies[apart].wait_send()
 
@@ -463,17 +868,78 @@
     )(qz, kv)
 
 
-def attend_back(qz, kv, rk, d_attn, attn_t, bound, levels):
+def middle(attn, w_out, tokens, gain, w_up, w_down, cotangent):
+    rows, width = tokens.shape
+    units = w_up.shape[1]
+    own = rows // 4
+    sub = own // PARTS
+    parts = lambda *dims: pltpu.VMEM((PARTS,) + dims + (sub, width), bf16)
+    return pl.pallas_call(
+        middle_kernel,
+        out_shape=(
+            shape(attn.shape, bf16),
+            shape((own, width), f32),
+            shape((own, width), f32),
+            shape((1, 2, 2, own, width), bf16),
+            shape(w_out.shape, bf16),
+            shape(w_up.shape, bf16),
+            shape(w_down.shape, bf16),
+            shape((1, width), f32),
+        ),
+        in_specs=[VMEM] * 7,
+        out_specs=(VMEM,) * 8,
+        scratch_shapes=[
+            pltpu.VMEM(attn.shape, bf16),
+            pltpu.VMEM((rows, units), bf16),
+            pltpu.VMEM((rows, units), f32),
+            pltpu.VMEM((rows, units), bf16),
+            parts(2, 2), parts(2, 2),
+            parts(2, 2), parts(2), parts(), parts(),
+            parts(2, 2), parts(2), parts(), parts(),
+            pltpu.SemaphoreType.DMA((2, 10, PARTS)),
+        ],
+        compiler_params=pltpu.CompilerParams(
+            vmem_limit_bytes=LIMIT, collective_id=2, has_side_effects=True
+        ),
+    )(attn, w_out, tokens, gain.reshape(1, -1), w_up, w_down, cotangent)
+
+
+def back(levels, bits, qz, kv, rk, d_attn, attn_t, bound, mid, gain, tokens, normed, w_qkv):
+    middle_own, d_middle, mlp, part_out, part_up, part_down, part_gain = mid
     heads, rows, _ = kv.shape
     half = rows // 2
+    own = rows // 4
+    sub = own // PARTS
+    width = tokens.shape[1]
+    wide = heads * SLOT
     peers = (1 << levels) - 1
+    orders = (list(range(bits)), [1, 0][:bits] + list(range(2, bits))) if bits > 1 else ([0], [0])
+    halvings = min(2, bits - 1)
+
+    def landing(dims):
+        total, size = 0, dims[-2]
+        for step in range(bits):
+            size = size // 2 if step < halvings else size
+            total += size
+        return pltpu.VMEM(dims[:-2] + (total, dims[-1]), bf16)
+
+    parts = lambda *dims: pltpu.VMEM((PARTS,) + dims + (sub, width), bf16)
+    qkv_dims = w_qkv.shape
     return pl.pallas_call(
-        partial(attend_back_kernel, levels, heads),
-        out_shape=shape((3, rows, heads * HD), bf16),
-        in_specs=[VMEM] * 6,
-        out_specs=VMEM,
+        partial(back_kernel, levels, heads, orders),
+        out_shape=(
+            shape((rows, width), bf16),
+            shape((rows, width), bf16),
+            shape(part_out.shape, bf16),
+            shape(part_up.shape, bf16),
+            shape(part_down.shape, bf16),
+            shape(qkv_dims, bf16),
+            shape((8, width), f32),
+        ),
+        in_specs=[VMEM] * 17,
+        out_specs=(VMEM,) * 7,
         scratch_shapes=[
-            pltpu.VMEM((rows, heads * SLOT), bf16),
+            pltpu.VMEM((rows, wide), bf16),
             pltpu.VMEM((heads, rows, 128), bf16),
             pltpu.VMEM((heads, 1, rows), f32),
             pltpu.VMEM((heads, SLOT, rows), bf16),
@@ -484,20 +950,33 @@
             pltpu.VMEM((heads // 2, rows, 128), f32),
             pltpu.VMEM((heads, levels * half, 128), bf16),
             pltpu.VMEM((heads, levels * half, 128), bf16),
-            pltpu.VMEM((3, rows, heads * SLOT), bf16),
+            pltpu.VMEM((3, rows, wide), bf16),
+            pltpu.VMEM((3, rows, heads * HD), bf16),
+            pltpu.VMEM((1, 2, own, width), bf16),
+            pltpu.VMEM((1, own, width), bf16),
+            pltpu.VMEM((1, own, width), bf16),
+            parts(2, 2), parts(2), parts(), parts(),
+            pltpu.VMEM(part_out.shape, bf16),
+            pltpu.VMEM(part_up.shape, bf16),
+            pltpu.VMEM(part_down.shape, bf16),
+            pltpu.VMEM(qkv_dims, bf16),
+            landing(part_out.shape), landing(part_up.shape), landing(part_down.shape), landing(qkv_dims),
+            pltpu.VMEM((bits + 3, 8, width), f32),
+            pltpu.VMEM((bits + 2, 8, width), f32),
             pltpu.SemaphoreType.DMA((peers,)),
             pltpu.SemaphoreType.DMA((peers,)),
+            pltpu.SemaphoreType.DMA((2, 5, 1)),
+            pltpu.SemaphoreType.DMA((2, 5, PARTS)),
+            pltpu.SemaphoreType.DMA((2, 6, bits + 2)),
+            pltpu.SemaphoreType.DMA((2, bits + 2)),
         ],
         compiler_params=pltpu.CompilerParams(
             vmem_limit_bytes=LIMIT, collective_id=1, has_side_effects=True
         ),
-    )(qz, kv, rk, d_attn, attn_t, bound)
-
-
-def normalize(rows_in, gain):
-    centre = rows_in - jnp.mean(rows_in, axis=-1, keepdims=True)
-    spread = jnp.mean(centre * centre, axis=-1, keepdims=True)
-    return centre * lax.rsqrt(spread + EPS) * gain
+    )(
+        qz, kv, rk, d_attn, attn_t, bound, middle_own, d_middle, mlp, part_out, part_up, part_down,
+        part_gain, tokens, gain.reshape(1, -1), normed, w_qkv,
+    )
 
 
 def mask_columns(slide_ids, valid, wide):
@@ -513,44 +992,20 @@
 
 def body(tokens, slide_ids, valid, norm_one, w_qkv, w_out, norm_two, w_up, w_down, cotangent):
     heads = w_out.shape[0] // HD
-    levels = level_count(lax.axis_size("seq"))
-    first = tokens.astype(f32)
+    n_seq = lax.axis_size("seq")
+    levels = level_count(n_seq)
     aux = mask_columns(slide_ids, valid, heads * SLOT)
-    normed_low, qz, kv = project(tokens, aux, norm_one, w_qkv, heads)
+    w_turned = jnp.swapaxes(w_qkv, 1, 2)
+    normed, qz, kv = project(tokens, aux, norm_one, w_turned, heads)
     attn_low, attn_t, bound, rk = attend(qz, kv, levels)
-    attn_term = jnp.dot(attn_low, w_out, preferred_element_type=f32)
-    middle = first + lax.psum(attn_term.astype(bf16), "head").astype(f32)
-    second, pull_two = jax.vjp(normalize, middle, norm_two)
-    second_low = second.astype(bf16)
-    up_proj = jnp.dot(second_low, w_up, preferred_element_type=f32)
-    hidden, pull_gelu = jax.vjp(partial(jax.nn.gelu, approximate=False), up_proj)
-    hidden_low = hidden.astype(bf16)
-    mlp_term = jnp.dot(hidden_low, w_down, preferred_element_type=f32)
-    output = (middle + lax.psum(mlp_term.astype(bf16), "head").astype(f32)).astype(bf16)
-    grad_down = jnp.einsum("tf,td->fd", hidden_low, cotangent, preferred_element_type=f32)
-    d_hidden = jnp.einsum("td,fd->tf", cotangent, w_down, preferred_element_type=f32)
-    d_up = pull_gelu(d_hidden)[0].astype(bf16)
-    grad_up = jnp.einsum("td,tf->df", second_low, d_up, preferred_element_type=f32)
-    d_second_term = jnp.einsum("tf,df->td", d_up, w_up, preferred_element_type=f32)
-    d_second = lax.psum(d_second_term.astype(bf16), "head").astype(f32)
-    d_middle_norm, grad_norm_two = pull_two(d_second)
-    d_middle = cotangent.astype(f32) + d_middle_norm
-    d_branch = d_middle.astype(bf16)
-    grad_out = jnp.einsum("te,td->ed", attn_low, d_branch, preferred_element_type=f32)
-    d_attn = jnp.einsum("td,ed->te", d_branch, w_out, preferred_element_type=f32).astype(bf16)
-    early = lax.psum(tuple(g.astype(bf16) for g in (grad_out, grad_up, grad_down)), "seq")
-    d_mixed = attend_back(qz, kv, rk, d_attn, attn_t, bound, levels)
-    grad_qkv = jnp.einsum("td,cte->cde", normed_low, d_mixed, preferred_element_type=f32)
-    d_normed_term = jnp.einsum("cte,cde->td", d_mixed, w_qkv, preferred_element_type=f32)
-    d_normed = lax.psum(d_normed_term.astype(bf16), "head").astype(f32)
-    pull_one = jax.vjp(normalize, first, norm_one)[1]
-    d_first, grad_norm_one = pull_one(d_normed)
-    input_grad = d_middle + d_first
-    norms = lax.psum(jnp.stack([grad_norm_one, grad_norm_two]), "seq")
-    late = lax.psum(grad_qkv.astype(bf16), "seq")
+    d_attn, *mid = middle(attn_low, w_out, tokens, norm_two, w_up, w_down, cotangent)
+    output, input_grad, grad_out, grad_up, grad_down, grad_qkv, gains = back(
+        levels, n_seq.bit_length() - 1, qz, kv, rk, d_attn, attn_t, bound, mid,
+        norm_one, tokens, normed, w_turned,
+    )
     return (
-        output, input_grad, norms[0], late.astype(f32), early[0].astype(f32), norms[1],
-        early[1].astype(f32), early[2].astype(f32),
+        output, input_grad.astype(f32), gains[0], jnp.swapaxes(grad_qkv, 1, 2).astype(f32),
+        grad_out.astype(f32), gains[1], grad_up.astype(f32), grad_down.astype(f32),
     )
 
 

time: 468 us -> 263 us (0.56); the launches traced: 461 us -> 262 us
  waiting for transfers between devices: 247 us -> 0 us
  Pallas kernels: 95.7 us -> 243 us
  matrix products: 33.7 us -> 0 us
  blocking collectives: 23 us -> 0 us
  other arithmetic: 35.3 us -> 13 us
  between operations: 14.6 us -> 0.68 us
  local copies, waits for them, and re-layouts: 11.1 us -> 5.8 us
    psum x4 -> x0, waiting for transfers between devices: 247 us -> none  [the longest x1 109 us: body(): late = lax.psum(grad_qkv.astype(bf16), 'seq')]
    pallas_call x1 -> x2, Pallas kernels: 45 us -> 192 us  [the longest x1 140 us: back(): pl.pallas_call(partial(back_kernel, levels, heads, orders), out_shape=(sh...]
    dot_general x11 -> x0, matrix products: 33.7 us -> none  [the longest x1 9.37 us: body(): jnp.einsum('td,fd->tf', cotangent, w_down, preferred_element_type=f32)]
    psum x1 -> x0, blocking collectives: 23 us -> none  [body(): norms = lax.psum(jnp.stack([grad_norm_one, grad_norm_two]), 'seq')]
    reduce_sum x6 -> x0, other arithmetic: 13.4 us -> none  [the longest x2 6.2 us: normalize(): return centre * lax.rsqrt(spread + EPS) * gain]
    unnamed x55 -> x9, local copies, waits for them, and re-layouts: 8.24 us -> 1.84 us
    add x1 -> x0, other arithmetic: 6.11 us -> none  [body(): input_grad = d_middle + d_first]
    convert_element_type x7 -> x5, other arithmetic: 12.1 us -> 9.48 us  [the longest x1 2.52 us: body(): jnp.swapaxes(grad_qkv, 1, 2).astype(f32)]
  transfers between devices with their start and end apart: 4 -> 0, of which waited for: 4 -> 0; matrix products, arithmetic and copies ran while one was open for 6% -> 0% of each run, Pallas kernels for 0% -> 0%
where the time goes in v2:
time: 263 us; the launch traced here: 262 us
  Pallas kernels  243 us (92%)
  other arithmetic  13 us (5%)
  local copies, waits for them, and re-layouts  5.8 us (2%)
    pallas_call x1, Pallas kernels, back(): pl.pallas_call(partial(back_kernel, levels, heads, orders), out_shape=(sh...  140 us
    pallas_call x1, Pallas kernels, middle(): pl.pallas_call(middle_kernel, out_shape=(shape(attn.shape, bf16), shape((...  52.8 us
    pallas_call x1, Pallas kernels, attend(): pl.pallas_call(partial(attend_kernel, levels, heads), out_shape=(shape((r...  39.1 us
    pallas_call x1, Pallas kernels, project(): pl.pallas_call(partial(project_kernel, heads), out_shape=(shape((rows, wi...  11.3 us

profile of v2, /device:TPU:0, one launch (start us, length us, event | category | flops | bytes accessed | tf_op | source)
XLA Modules:
  0.0 262.2 jit_solution(16192951337832596714)
XLA Ops:
  0.7 0.7 broadcast_compare_fusion.1
  1.4 1.3 reshape.60.gain_ref
  2.6 1.3 reshape.61.gain_ref
  3.9 2.8 %select_convert_fusion.aux_ref = bf16[1024,512]{1,0:T(8,128)(2,1)} fusion(s32[512]{0:T(512)S(1)} %fusion, s32[1024]{0:T(1024)} %param.11, pred[512]{0:T(512)(128)(4,1)S(1)} %broadcast_compare_fusion.2, pred[512]{0:T(512)(128)(4,1)S(1)} %get-tuple-element.57, pred[512]{0:T(512)(128)(4,1)S(1)} %get-tuple-element.56, pred[1024]{0:T(1024)(128)(4,1)S(1)} %get-tuple-element.55, ...), kind=kLoop, calls=%fused_computation | loop fusion | flops 6291456 | bytes 1058304 | tf_op jit(solution)/shard_map/convert_element_type | solution.py:990
  6.7 11.3 %shard_map.161 = (bf16[1024,768]{1,0:T(8,128)(2,1)}, bf16[4,1024,128]{2,1,0:T(8,128)(2,1)}, bf16[4,1024,128]{2,1,0:T(8,128)(2,1)}) custom-call(bf16[1024,768]{1,0:T(8,128)(2,1)} %tokens_ref.5, bf16[1024,512]{1,0:T(8,128)(2,1)} %select_convert_fusion.aux_ref, f32[1,768]{1,0:T(1,128)} %reshape.60.gain_ref, bf16[3,192,768]{2,1,0:T(8,128)(2,1)} %bitcast.3), custom_call_target="tpu_custom_call" | custom-call | tf_op jit(solution)/shard_map/pallas_call | solution.py:826
  18.0 39.1 %shard_map.162 = (bf16[1024,192]{1,0:T(8,128)(2,1)}, f32[4,64,1024]{2,1,0:T(8,128)}, f32[4,1,1024]{2,1,0:T(1,128)}, bf16[4,1536,128]{2,1,0:T(8,128)(2,1)}) custom-call(bf16[4,1024,128]{2,1,0:T(8,128)(2,1)} %get-tuple-element.30.qz_ref, bf16[4,1024,128]{2,1,0:T(8,128)(2,1)} %get-tuple-element.31.kv_ref), custom_call_target="tpu_custom_call" | custom-call | tf_op jit(solution)/shard_map/pallas_call | solution.py:844
  57.1 52.8 %shard_map.163 = (bf16[1024,192]{1,0:T(8,128)(2,1)}, f32[256,768]{1,0:T(8,128)}, f32[256,768]{1,0:T(8,128)}, bf16[1,2,2,256,768]{4,3,2,1,0:T(8,128)(2,1)}, bf16[...) custom-call(bf16[1024,192]{1,0:T(8,128)(2,1)} %get-tuple-element.33.attn_ref, ...), custom_call_target="tpu_custom_call" | custom-call | tf_op jit(solution)/shard_map/pallas_call | solution.py:877
  109.8 139.7 %shard_map.164 = (bf16[1024,768]{1,0:T(8,128)(2,1)}, bf16[1024,768]{1,0:T(8,128)(2,1)}, bf16[192,768]{1,0:T(8,128)(2,1)}, bf16[768,768]{1,0:T(8,128)(2,1)}, bf16...) custom-call(bf16[4,1024,128]{2,1,0:T(8,128)(2,1)} %get-tuple-element.30.qz_ref, ...), custom_call_target="tpu_custom_call" | custom-call | tf_op jit(solution)/shard_map/pallas_call | solution.py:928
  249.5 1.4 slice_reduce_fusion
  250.9 0.0 copy-start.3
  250.9 1.9 convert_element_type.25
  252.8 2.5 convert_bitcast_fusion
  255.3 0.0 copy-done.3
  255.4 0.0 copy-start.2
  255.4 1.6 convert_element_type.26
  256.9 0.1 copy-done.2
  257.0 0.0 copy-start.1
  257.0 1.6 convert_element_type.27
  258.6 0.5 copy-done.1
  259.1 0.0 copy-start
  259.1 1.9 convert_element_type.22
  261.0 0.1 copy-done
  261.1 1.1 copy.19
  (3 shorter events, 0.0 us)
Async XLA Ops:
  250.9 4.4 %copy-start.3 = (bf16[768,768]{1,0:T(8,128)(2,1)S(1)}, bf16[768,768]{1,0:T(8,128)(2,1)}, u32[]{:S(2)}) copy-start(bf16[768,768]{1,0:T(8,128)(2,1)} %get-tuple-element.50) | copy-start | bytes 3538948
  255.4 1.7 copy-start.2
  257.0 2.1 copy-start.1
  259.1 2.0 copy-start

commit v3 on v2

--- a/solution.py
+++ b/solution.py
@@ -110,8 +110,9 @@
     pl.semaphore_wait(barrier, len(peers))
 
 
-def seq_sum(me, src, out, buf, sem, slot, order):
-    lo, size, offset, halved, sent = 0, src.shape[0], 0, [], []
+def seq_sum(me, src, out, buf, sem, slot, order, part=0, parts=1):
+    size, offset = src.shape[0] // parts, buf.shape[0] // parts * part
+    lo, halved, sent = size * part, [], []
     halvings = min(2, len(order) - 1)
     for step, bit in enumerate(order):
         mine = me // (1 << bit) % 2
@@ -637,11 +638,16 @@
     src_up_ref[...] = part_up_ref[...]
     src_down_ref[...] = part_down_ref[...]
     src_out_ref[...] = part_out_ref[...]
-    ups = seq_sum(me, src_up_ref, grad_up_ref, buf_up_ref, seq_sem, 0, orders[0])
-    downs = seq_sum(me, src_down_ref, grad_down_ref, buf_down_ref, seq_sem, 1, orders[1])
-    outs = seq_sum(me, src_out_ref, grad_out_ref, buf_out_ref, seq_sem, 2, orders[0])
+    u0, u1 = [
+        seq_sum(me, src_up_ref, grad_up_ref, buf_up_ref, seq_sem, k, orders[0], k, 2) for k in range(2)
+    ]
+    d0, d1 = [
+        seq_sum(me, src_down_ref, grad_down_ref, buf_down_ref, seq_sem, 2 + k, orders[k], k, 2)
+        for k in range(2)
+    ]
+    outs = seq_sum(me, src_out_ref, grad_out_ref, buf_out_ref, seq_sem, 4, orders[0])
     mlp_sum.start(0)
-    pump(ups, downs)
+    pump(u0, d1, u1, d0, outs)
 
     swap = digit_swap()
     spread = spreader(width)
@@ -665,6 +671,7 @@
         turned = dot_nt(unit, doz_ref[h])[h % 2 * SLOT : h % 2 * SLOT + SLOT]
         delta_ref[h] = jnp.sum(turned * attn_t_ref[h], axis=0, keepdims=True)
     mlp_sum.forward(0)
+    pump(u0, d1)
 
     dqt_ref[...] = jnp.zeros_like(dqt_ref)
     copies = {}
@@ -701,43 +708,44 @@
                 device_id_type=MESH,
             )
             copies[apart].start()
+        if level == 0:
+            pump(u0, u1)
 
     output_ref[mine_of(0, own), :] = (middle_ref[...] + mlp_sum.total(0)).astype(bf16)
     outputs.start(0)
-    pump(ups, downs, outs)
+    pump(u1, d0)
     transpose_heads(kv_ref, 0, 0, rows, kt_ref, heads)
 
-    def local(pair, carry):
+    def local(pair, qt):
         counts = pair_counts(half, half, half, None)
-        for qt in range(2):
-            there = slice(qt * half, qt * half + half)
-            for side in range(2):
-                h = 2 * pair + side
-                q, do = qz_ref[h, there, :], doz_ref[h, there, :]
-                for kt in range(2):
-                    keys = slice(kt * half, kt * half + half)
-                    p = jnp.exp2(dot_nt(kv_ref[pair, keys, :], q) - bound_ref[h, :, there])
-                    if qt == 0 and kt == 0:
-                        p = p * counts
-                    ds = p * (dot_nt(kv_ref[pairs + pair, keys, :], do) - delta_ref[h, :, there])
-                    p_ref[side, keys, :] = p.astype(bf16)
-                    ds_ref[side, keys, :] = ds.astype(bf16)
-                dv = dot(p_ref[side], do)
-                dk = dot(ds_ref[side], q)
-                if qt == 0 and side == 0:
-                    dkv_ref[pairs + pair] = dv
-                    dkv_ref[pair] = dk
-                else:
-                    dkv_ref[pairs + pair] += dv
-                    dkv_ref[pair] += dk
-                dqt_ref[h, :, there] += dot(kt_ref[h], ds_ref[side])
-        return carry
-
-    for pair in range(pairs):
-        local(pair, 0)
-        if pair == 0:
+        there = slice(qt * half, qt * half + half)
+        for side in range(2):
+            h = 2 * pair + side
+            q, do = qz_ref[h, there, :], doz_ref[h, there, :]
+            for kt in range(2):
+                keys = slice(kt * half, kt * half + half)
+                p = jnp.exp2(dot_nt(kv_ref[pair, keys, :], q) - bound_ref[h, :, there])
+                if qt == 0 and kt == 0:
+                    p = p * counts
+                ds = p * (dot_nt(kv_ref[pairs + pair, keys, :], do) - delta_ref[h, :, there])
+                p_ref[side, keys, :] = p.astype(bf16)
+                ds_ref[side, keys, :] = ds.astype(bf16)
+            dv = dot(p_ref[side], do)
+            dk = dot(ds_ref[side], q)
+            if qt == 0 and side == 0:
+                dkv_ref[pairs + pair] = dv
+                dkv_ref[pair] = dk
+            else:
+                dkv_ref[pairs + pair] += dv
+                dkv_ref[pair] += dk
+            dqt_ref[h, :, there] += dot(kt_ref[h], ds_ref[side])
+
+    turns = [(u0, outs, d1), (u1, d0), (u0, d1), (u1, d0, outs)]
+    for turn in range(2 * pairs):
+        local(turn // 2, turn % 2)
+        if turn == 1:
             outputs.relay(0)
-        pump(ups, downs, outs)
+        pump(*turns[turn % 4])
     for pair in range(pairs):
         dq_ref[pair] = (
             jnp.concatenate([dqt_ref[2 * pair], dqt_ref[2 * pair + 1]], axis=0) * (1.0 / LOG2E)
@@ -749,8 +757,10 @@
     for pair in range(pairs):
         dkv_ref[pair] = dkv_ref[pair] * FACTOR
     from_heads([(dq_ref, pair) for pair in range(pairs)], base, d_ref.at[0], block)
+    pump(outs, d1)
     from_heads([(dkv_ref.at[:pairs], pair) for pair in range(pairs)], base, d_ref.at[1], block)
     from_heads([(dkv_ref.at[pairs:], pair) for pair in range(pairs)], base, d_ref.at[2], block)
+    pump(d0, outs)
     unspread = unspreader(width)
 
     def natural(k, carry):
@@ -782,7 +792,7 @@
     for c in range(3):
         src_qkv_ref[c] = dot_tn(dm_ref[c], normed_ref[...]).astype(bf16)
     qkvs = [
-        seq_sum(me, src_qkv_ref.at[c], grad_qkv_ref.at[c], buf_qkv_ref.at[c], seq_sem, 3 + c, orders[c % 2])
+        seq_sum(me, src_qkv_ref.at[c], grad_qkv_ref.at[c], buf_qkv_ref.at[c], seq_sem, 5 + c, orders[c % 2])
         for c in range(3)
     ]
     pump(*qkvs)
@@ -802,10 +812,12 @@
     each(rows_back)
     bits = [("head", 0), ("head", 1)] + [("seq", bit) for bit in orders[0]]
     gains = gain_sum(bits, gain_mine_ref, gain_got_ref, gain_sem)
-    pump(ups, downs, outs, gains, *qkvs)
-    each(inputs.relay)
+    pump(gains)
+    for s in range(PARTS):
+        pump(*qkvs, gains)
+        inputs.relay(s)
     for _ in range(2 * len(bits) + 4):
-        pump(gains, ups, downs, outs, *qkvs)
+        pump(gains, u0, u1, d1, d0, outs, *qkvs)
     gains_ref[...] = gain_mine_ref[len(bits)]
     each(inputs.arrive)
     outputs.arrive(0)
@@ -967,7 +979,7 @@
             pltpu.SemaphoreType.DMA((peers,)),
             pltpu.SemaphoreType.DMA((2, 5, 1)),
             pltpu.SemaphoreType.DMA((2, 5, PARTS)),
-            pltpu.SemaphoreType.DMA((2, 6, bits + 2)),
+            pltpu.SemaphoreType.DMA((2, 8, bits + 2)),
             pltpu.SemaphoreType.DMA((2, bits + 2)),
         ],
         compiler_params=pltpu.CompilerParams(

time: 263 us -> 248 us (0.943)
  Pallas kernels: 243 us -> 228 us
    pallas_call x1, Pallas kernels: 140 us -> 125 us  [back(): pl.pallas_call(partial(back_kernel, levels, heads, orders), out_shape=(sh...]
where the time goes in v3:
time: 248 us
  Pallas kernels  228 us (92%)
  other arithmetic  13 us (5%)
  local copies, waits for them, and re-layouts  5.8 us (2%)
    pallas_call x1, Pallas kernels, back(): pl.pallas_call(partial(back_kernel, levels, heads, orders), out_shape=(sh...  125 us
    pallas_call x1, Pallas kernels, middle(): pl.pallas_call(middle_kernel, out_shape=(shape(attn.shape, bf16), shape((...  52.8 us
    pallas_call x1, Pallas kernels, attend(): pl.pallas_call(partial(attend_kernel, levels, heads), out_shape=(shape((r...  39.1 us
    pallas_call x1, Pallas kernels, project(): pl.pallas_call(partial(project_kernel, heads), out_shape=(shape((rows, wi...  11.3 us

profile of v3, /device:TPU:0, one launch (start us, length us, event | category | flops | bytes accessed | tf_op | source)
XLA Modules:
  0.0 247.7 jit_solution(17700838717988835926)
XLA Ops:
  0.7 0.7 broadcast_compare_fusion.1
  1.4 1.3 reshape.60.gain_ref
  2.6 1.3 reshape.61.gain_ref
  3.9 2.8 %select_convert_fusion.aux_ref = bf16[1024,512]{1,0:T(8,128)(2,1)} fusion(s32[512]{0:T(512)S(1)} %fusion, s32[1024]{0:T(1024)} %param.11, pred[512]{0:T(512)(128)(4,1)S(1)} %broadcast_compare_fusion.2, pred[512]{0:T(512)(128)(4,1)S(1)} %get-tuple-element.57, pred[512]{0:T(512)(128)(4,1)S(1)} %get-tuple-element.56, pred[1024]{0:T(1024)(128)(4,1)S(1)} %get-tuple-element.55, ...), kind=kLoop, calls=%fused_computation | loop fusion | flops 6291456 | bytes 1058304 | tf_op jit(solution)/shard_map/convert_element_type | solution.py:1002
  6.7 11.3 %shard_map.161 = (bf16[1024,768]{1,0:T(8,128)(2,1)}, bf16[4,1024,128]{2,1,0:T(8,128)(2,1)}, bf16[4,1024,128]{2,1,0:T(8,128)(2,1)}) custom-call(bf16[1024,768]{1,0:T(8,128)(2,1)} %tokens_ref.5, bf16[1024,512]{1,0:T(8,128)(2,1)} %select_convert_fusion.aux_ref, f32[1,768]{1,0:T(1,128)} %reshape.60.gain_ref, bf16[3,192,768]{2,1,0:T(8,128)(2,1)} %bitcast.3), custom_call_target="tpu_custom_call" | custom-call | tf_op jit(solution)/shard_map/pallas_call | solution.py:838
  18.0 39.1 %shard_map.162 = (bf16[1024,192]{1,0:T(8,128)(2,1)}, f32[4,64,1024]{2,1,0:T(8,128)}, f32[4,1,1024]{2,1,0:T(1,128)}, bf16[4,1536,128]{2,1,0:T(8,128)(2,1)}) custom-call(bf16[4,1024,128]{2,1,0:T(8,128)(2,1)} %get-tuple-element.30.qz_ref, bf16[4,1024,128]{2,1,0:T(8,128)(2,1)} %get-tuple-element.31.kv_ref), custom_call_target="tpu_custom_call" | custom-call | tf_op jit(solution)/shard_map/pallas_call | solution.py:856
  57.1 52.8 %shard_map.163 = (bf16[1024,192]{1,0:T(8,128)(2,1)}, f32[256,768]{1,0:T(8,128)}, f32[256,768]{1,0:T(8,128)}, bf16[1,2,2,256,768]{4,3,2,1,0:T(8,128)(2,1)}, bf16[...) custom-call(bf16[1024,192]{1,0:T(8,128)(2,1)} %get-tuple-element.33.attn_ref, ...), custom_call_target="tpu_custom_call" | custom-call | tf_op jit(solution)/shard_map/pallas_call | solution.py:889
  109.8 125.2 %shard_map.164 = (bf16[1024,768]{1,0:T(8,128)(2,1)}, bf16[1024,768]{1,0:T(8,128)(2,1)}, bf16[192,768]{1,0:T(8,128)(2,1)}, bf16[768,768]{1,0:T(8,128)(2,1)}, bf16...) custom-call(bf16[4,1024,128]{2,1,0:T(8,128)(2,1)} %get-tuple-element.30.qz_ref, ...), custom_call_target="tpu_custom_call" | custom-call | tf_op jit(solution)/shard_map/pallas_call | solution.py:940
  235.0 1.4 slice_reduce_fusion
  236.4 0.0 copy-start.3
  236.4 1.9 convert_element_type.25
  238.3 2.5 %convert_bitcast_fusion = f32[3,768,192]{1,2,0:T(8,128)} fusion(bf16[3,192,768]{2,1,0:T(8,128)(2,1)} %get-tuple-element.48), kind=kLoop, calls=%fused_computation.1 | loop fusion | flops 442368 | bytes 2654208 | tf_op jit(solution)/shard_map/convert_element_type | solution.py:1019
  240.9 0.0 copy-done.3
  240.9 0.0 copy-start.2
  240.9 1.6 convert_element_type.26
  242.4 0.1 copy-done.2
  242.5 0.0 copy-start.1
  242.5 1.6 convert_element_type.27
  244.1 0.5 copy-done.1
  244.7 0.0 copy-start
  244.7 1.9 convert_element_type.22
  246.6 0.1 copy-done
  246.6 1.1 copy.19
  (3 shorter events, 0.0 us)
Async XLA Ops:
  236.4 4.4 %copy-start.3 = (bf16[768,768]{1,0:T(8,128)(2,1)S(1)}, bf16[768,768]{1,0:T(8,128)(2,1)}, u32[]{:S(2)}) copy-start(bf16[768,768]{1,0:T(8,128)(2,1)} %get-tuple-element.50) | copy-start | bytes 3538948
  240.9 1.7 copy-start.2
  242.5 2.1 copy-start.1
  244.7 2.0 copy-start
